TPU v7x, 256 devices: a whole 4x4x8 slice. The times are simulated.
256 devices in a mesh: section: 8 (over z), expert: 16 (over y, x), dp: 2 (over core).
Axes of the slice: x: 4, y: 4, z: 8, core: 2. Of those that a mesh axis runs over, the one named last changes fastest.
Arguments:
- stash: bfloat16 [8, 256, 2048], P('section', 'dp', 'expert'), may hold values from -6 to 6
- cotangent: bfloat16 [8, 256, 2048], P('section', 'dp', 'expert'), may hold values from -6 to 6
- backward_expert_routes: int32 [8, 256, 2], P('section', 'dp'), may hold values from 0 to 3, all different within a row; in each aligned block of 128 rows (0 to 127, 128 to 255, ..., all dimensions but the last counted through in order) at most 80 rows name the same one
- backward_job_lengths: int32 [8, 4], P('section'), may hold values from 1 to 128, 256 in all within a row
- layer_norm_gains: float32 [8, 2048], P('section'), may hold values from 0.25 to 1.75
- router: bfloat16 [8, 2048, 4], P('section'), may hold values from -0.125 to 0.125
- expert_gate_weight: bfloat16 [8, 2048, 28672], P('section', None, ('expert', 'dp')), may hold values from -0.125 to 0.125
- expert_up_weight: bfloat16 [8, 2048, 28672], P('section', None, ('expert', 'dp')), may hold values from -0.125 to 0.125
- expert_down_weight: bfloat16 [8, 28672, 2048], P('section', ('expert', 'dp')), may hold values from -0.0625 to 0.0625
- adapter_down_maps: bfloat16 [8, 2048, 64], P('section', 'expert'), may hold values from -0.125 to 0.125
- adapter_up_maps: bfloat16 [8, 64, 2048], P('section', None, 'expert'), may hold values from -1.5 to 1.5
Outputs:
- handed_back: bfloat16 [8, 256, 2048], P('section', 'dp', 'expert')
- grad_lora_down: float32 [8, 2048, 64], P('section', 'expert')
- grad_lora_up: float32 [8, 64, 2048], P('section', None, 'expert')
Inputs may be any that keep to these rules, and one draw needn't show every extreme that they name: `backward_expert_routes`: each row names two different experts. In each aligned block of 128 rows (the tokens of one device) no expert is named more than 80 times. `backward_job_lengths`: each row sums to 256.
All inputs are finite; a program needn't handle non-finite values.
Results may differ from a plain program's by a relative error of at most 0.008.
Values may be sent and summed in bfloat16 or wider, within the bound.
No kernel may reach another device: no remote copies, remote signals or barrier semaphores. Data moves between devices by JAX's collectives and lax.ppermute only.
A program may use at most 64 MiB of HBM per device.

v0:
```python
import jax
import jax.numpy as jnp
from jax import lax
from jax.sharding import Mesh
from jax.sharding import PartitionSpec as P

MODEL_WIDTH = 2048
EXPERTS = 4
ADAPTER_RANK = 16
CAP = 80
EXPERT = ("expert_0", "expert_1")
EXPERT_DP = ("expert_0", "expert_1", "dp")


EPS = 1e-05
ADAPTER_SCALE = 0.5


def in_one_piece(arrays, axis, dim, along):
    ends, at = ([], 0)
    for a in arrays[:-1]:
        at += a.shape[along]
        ends.append(at)
    both = jnp.concatenate(arrays, axis=along)
    return tuple(jnp.split(lax.all_gather(both, axis, axis=dim, tiled=True), ends, axis=along))


def laid_out(blocks, dim):
    blocks = jnp.moveaxis(blocks, 0, dim)
    dims = blocks.shape
    return blocks.reshape(*dims[:dim], dims[dim] * dims[dim + 1], *dims[dim + 2 :])


def from_everyone(x, axis):
    devices = lax.axis_size(axis)
    return lax.all_to_all(jnp.broadcast_to(x[None], (devices, *x.shape)), axis, 0, 0, tiled=True)


def collect(x, axis, dim):
    return laid_out(from_everyone(x, axis), dim)


def of_everyone(x, axis):
    return from_everyone(x, axis).sum(axis=0)


def packed_total(arrays, axis):
    line, at, finished = (jnp.concatenate([a.reshape(-1) for a in arrays]), 0, [])
    total = of_everyone(line, axis)
    for a in arrays:
        finished.append(total[at : at + a.size].reshape(a.shape))
        at += a.size
    return tuple(finished)


def in_blocks(x, dim, devices):
    dims = x.shape
    blocks = x.reshape(*dims[:dim], devices, dims[dim] // devices, *dims[dim + 1 :])
    return jnp.moveaxis(blocks, dim, 0)


def sent_and_summed(x, axis, dim):
    blocks = in_blocks(x, dim, lax.axis_size(axis))
    arrived = lax.all_to_all(blocks, axis, split_axis=0, concat_axis=0, tiled=True)
    return arrived.sum(axis=0)


def in_one_piece_2(arrays, axis, dim, along):
    columns = [a.reshape(*a.shape[:along], -1) for a in arrays]
    both = jnp.concatenate(columns, axis=along)
    result, at, finished = (sent_and_summed(both, axis, dim), 0, [])
    for a, column in zip(arrays, columns):
        slab = result[..., at : at + column.shape[along]]
        finished.append(slab.reshape(*slab.shape[:along], *a.shape[along:]))
        at += column.shape[along]
    return tuple(finished)


def over_axes(x, axes):
    for axis in axes:
        x = lax.psum(x, axis)
    return x


def from_behind(block, axis, distance):
    devices = range(lax.axis_size(axis))
    route = [((i - distance) % len(devices), i) for i in devices]
    return lax.ppermute(block, axis, route)


def job_columns(job_token_lengths, offset, count):
    ends = jnp.cumsum(job_token_lengths, dtype=jnp.int32)
    position = offset + jnp.arange(count, dtype=jnp.int32)
    owner = jnp.sum((ends[None, :] <= position[:, None]).astype(jnp.int32), axis=1, dtype=jnp.int32)
    column_owner = (
        jnp.arange(job_token_lengths.shape[0] * ADAPTER_RANK, dtype=jnp.int32) // ADAPTER_RANK
    )
    return (owner[:, None] == column_owner[None, :]).astype(jnp.float32)


def prepare(whole_batch, norm_gain_vector, router, token_routes):
    expert_values = whole_batch.astype(jnp.float32)
    scale = lax.rsqrt(jnp.mean(expert_values * expert_values, axis=1, keepdims=True) + EPS)
    normalized_input = (expert_values * scale * norm_gain_vector[None, :]).astype(jnp.bfloat16)
    logits = jnp.dot(normalized_input, router, preferred_element_type=jnp.float32)
    labels = jnp.arange(router.shape[1], dtype=jnp.int32)
    first = (token_routes[:, 0:1] == labels[None, :]).astype(jnp.float32)
    second = (token_routes[:, 1:2] == labels[None, :]).astype(jnp.float32)
    upper = jax.nn.sigmoid(jnp.sum(first * logits, axis=1) - jnp.sum(second * logits, axis=1))
    table = upper[:, None] * first + (1.0 - upper)[:, None] * second
    return (expert_values, scale, normalized_input, first, second, upper, table)


def router_grad(gate_grad, first, second, upper):
    spread = jnp.sum(first * gate_grad, axis=1) - jnp.sum(second * gate_grad, axis=1)
    delta = spread * upper * (1.0 - upper)
    return delta[:, None] * (first - second)


def slot_matrix(member, capacity):
    marks = member.astype(jnp.int32)
    ranked = jnp.cumsum(marks, axis=-1, dtype=jnp.int32) - marks
    slots = jnp.arange(capacity, dtype=jnp.int32)
    hit = (ranked[..., None, :] == slots[:, None]) & (marks[..., None, :] == 1)
    return hit.astype(jnp.float32)


def expert_back(
    rows, adapter_gradient_list, expert_gate_weight, expert_up_weight, expert_down_weight
):
    gate = jnp.dot(rows, expert_gate_weight, preferred_element_type=jnp.float32)
    up = jnp.dot(rows, expert_up_weight, preferred_element_type=jnp.float32)
    sig = jax.nn.sigmoid(gate)
    act = gate * sig
    hidden = (act * up).astype(jnp.bfloat16)
    output = jnp.dot(hidden, expert_down_weight, preferred_element_type=jnp.float32)
    gate_term = jnp.sum(adapter_gradient_list.astype(jnp.float32) * output, axis=1)
    back = jnp.dot(adapter_gradient_list, expert_down_weight.T, preferred_element_type=jnp.float32)
    d_gate = (back * up * sig * (1.0 + gate * (1.0 - sig))).astype(jnp.bfloat16)
    d_up = (back * act).astype(jnp.bfloat16)
    d_rows = jnp.dot(d_gate, expert_gate_weight.T, preferred_element_type=jnp.float32) + jnp.dot(
        d_up, expert_up_weight.T, preferred_element_type=jnp.float32
    )
    return (d_rows, gate_term)


def shards(
    stash,
    cotangent,
    backward_expert_routes,
    backward_job_lengths,
    layer_norm_gains,
    router,
    expert_gate_weight,
    expert_up_weight,
    expert_down_weight,
    adapter_down_maps,
    adapter_up_maps,
):
    groups = lax.axis_size(EXPERT)
    column_block = lax.axis_index(EXPERT)
    token_block = lax.axis_index("dp")
    mine = column_block // (groups // EXPERTS)
    s_cols = stash[0]
    gradient_columns = cotangent[0]
    count, width = s_cols.shape
    s_full, g_full = in_one_piece((s_cols, gradient_columns), EXPERT, 1, 0)
    norm_gain_vector = layer_norm_gains[0]
    route_w = router[0]
    wg = expert_gate_weight[0]
    wu = expert_up_weight[0]
    wd = expert_down_weight[0]
    down_map_rows = adapter_down_maps[0]
    backward_columns = adapter_up_maps[0]
    col_start = column_block * width
    gain_cols = lax.dynamic_slice_in_dim(norm_gain_vector, col_start, width, 0)
    route_cols = lax.dynamic_slice_in_dim(route_w, col_start, width, 0)
    offset = token_block * count
    backward_mask = job_columns(backward_job_lengths[0], offset, count)
    b_values, b_scale, b_normed, b_first, b_second, b_upper, b_table = prepare(
        s_full, norm_gain_vector, route_w, backward_expert_routes[0]
    )
    labels = jnp.arange(EXPERTS, dtype=jnp.int32)
    own = (labels == mine).astype(jnp.float32)
    b_member = jnp.sum((b_first + b_second) * own[None, :], axis=1)
    b_gate = jnp.sum(b_table * own[None, :], axis=1)
    b_slots = slot_matrix(b_member, CAP)
    b_normed_cols = lax.dynamic_slice_in_dim(b_normed, col_start, width, 1)
    a_full = collect(down_map_rows, EXPERT, 0)
    b_low = jnp.dot(b_normed, a_full, preferred_element_type=jnp.float32)
    grad_low_rank = of_everyone(
        jnp.dot(gradient_columns, backward_columns.T, preferred_element_type=jnp.float32), EXPERT
    )
    backward_low_rank = (b_low * backward_mask).astype(jnp.bfloat16)
    grad_low_rank_backward = (ADAPTER_SCALE * grad_low_rank * backward_mask).astype(jnp.bfloat16)
    up_map_gradient = ADAPTER_SCALE * jnp.dot(
        backward_low_rank.T, gradient_columns, preferred_element_type=jnp.float32
    )
    down_map_gradient = jnp.dot(
        b_normed_cols.T, grad_low_rank_backward, preferred_element_type=jnp.float32
    )
    down_map_gradient, up_map_gradient = packed_total((down_map_gradient, up_map_gradient), "dp")
    normalized_grad_adapter = jnp.dot(
        grad_low_rank_backward, down_map_rows.T, preferred_element_type=jnp.float32
    )
    b_slots_low = b_slots.astype(jnp.bfloat16)
    b_sel = jnp.dot(b_slots_low, b_normed, preferred_element_type=jnp.float32).astype(jnp.bfloat16)
    g_sel = jnp.dot(b_slots_low, g_full, preferred_element_type=jnp.float32).astype(jnp.bfloat16)
    b_rows, g_rows = in_one_piece((b_sel, g_sel), "dp", 0, 1)
    dn_slots, dgam_slots = expert_back(b_rows, g_rows, wg, wu, wd)
    dn_own, dgam_own = in_one_piece_2((dn_slots, dgam_slots), "dp", 0, 1)
    b_term = jnp.dot((b_slots * b_gate[None, :]).T, dn_own)
    normalized_grad_experts = sent_and_summed(b_term, EXPERT, 1)
    dgam_tokens = jnp.dot(dgam_own, b_slots)
    gate_part = dgam_tokens[:, None] * own[None, :]
    expert_base_output = normalized_grad_experts + normalized_grad_adapter
    b_values_cols = lax.dynamic_slice_in_dim(b_values, col_start, width, 1)
    route_cols_t = route_cols.astype(jnp.float32).T
    gate_grad = over_axes(gate_part, EXPERT)
    d_logit = router_grad(gate_grad, b_first, b_second, b_upper)
    weighted = (expert_base_output + jnp.dot(d_logit, route_cols_t)) * gain_cols[None, :]
    stat = over_axes(jnp.sum(weighted * b_values_cols, axis=1, keepdims=True), EXPERT)
    layer_result = (
        gradient_columns.astype(jnp.float32)
        + b_scale * weighted
        - b_values_cols * b_scale * b_scale * b_scale * stat / MODEL_WIDTH
    )
    handed_back = from_behind(layer_result.astype(jnp.bfloat16), "section", -1)
    return (handed_back[None], down_map_gradient[None], up_map_gradient[None])


def solution(mesh):
    finer = Mesh(
        mesh.devices.reshape(mesh.shape["section"], 4, 4, mesh.shape["dp"]),
        ("section", "expert_0", "expert_1", "dp"),
    )
    in_specs = (
        P("section", "dp", EXPERT),
        P("section", "dp", EXPERT),
        P("section", "dp", None),
        P("section", None),
        P("section", None),
        P("section", None, None),
        P("section", None, EXPERT_DP),
        P("section", None, EXPERT_DP),
        P("section", EXPERT_DP, None),
        P("section", EXPERT, None),
        P("section", None, EXPERT),
    )
    out_specs = (P("section", "dp", EXPERT), P("section", EXPERT, None), P("section", None, EXPERT))
    return jax.shard_map(
        shards, mesh=finer, in_specs=in_specs, out_specs=out_specs, check_vma=False
    )
```

profile of v0, /device:TPU:10, one launch (start us, length us, event | category | flops | bytes accessed | tf_op | source)
XLA Modules:
  0.0 167.8 jit_solution(17074495569291303707)
XLA Ops:
  9.7 0.9 fusion.45
  10.6 0.9 broadcast_in_dim.10
  11.5 7.4 %all-to-all-start.2 = ((f32[16,128,64]{1,2,0:T(8,128)}), f32[16,128,64]{1,2,0:T(8,128)S(1)}, u32[]{:S(2)}, u32[]{:S(2)}) async-start(f32[16,128,64]{1,2,0:T(8,128)} %broadcast_in_dim.10), calls=%async_computation.2 | async-start | bytes 1048576 | tf_op jit(solution)/shard_map/all_to_all | solution.py:36
  19.2 40.3 %all-gather.3.cloned.1.call-done = bf16[256,2048]{0,1:T(8,128)(2,1)} async-done(((bf16[256,128]{0,1:T(8,128)(2,1)}), bf16[256,2048]{0,1:T(8,128)(2,1)}) %all-gather.3.cloned.1.call-update) | async-done | bytes 1048592 | tf_op jit(solution)/shard_map/all_gather | solution.py:25
  59.4 1.3 multiply_reduce_fusion
  60.8 1.5 multiply_convert_fusion
  63.6 0.9 pad_maximum_fusion.1
  65.4 6.9 %all-to-all-start.3 = ((bf16[16,128,64]{1,2,0:T(8,128)(2,1)}), bf16[16,128,64]{1,2,0:T(8,128)(2,1)S(1)}, u32[]{:S(2)}, u32[]{:S(2)}) async-start(bf16[16,128,64]{1,2,0:T(8,128)(2,1)} %broadcast_in_dim.13), calls=%async_computation.3 | async-start | bytes 524288 | tf_op jit(solution)/shard_map/all_to_all | solution.py:36
  72.6 5.3 %all-to-all-done.3 = bf16[16,128,64]{1,2,0:T(8,128)(2,1)S(1)} async-done(((bf16[16,128,64]{1,2,0:T(8,128)(2,1)}), bf16[16,128,64]{1,2,0:T(8,128)(2,1)S(1)}, u32[]{:S(2)}, u32[]{:S(2)}) %all-to-all-start.3) | async-done | bytes 262176 | tf_op jit(solution)/shard_map/all_to_all | solution.py:36
  78.3 3.8 %all_to_all.26 = f32[2,1,16384]{2,1,0:T(1,128)S(1)} all-to-all(f32[2,1,16384]{2,1,0:T(1,128)S(1)} %broadcast_in_dim.14), channel_id=1, replica_groups=mesh['section'=8,'expert_0'=4,'expert_1'=4,'dp'=2] {'dp'}, dimensions={0} | all-to-all | bytes 262144 | tf_op jit(solution)/shard_map/all_to_all | solution.py:36
  82.4 3.2 %fusion.2 = f32[160,896]{1,0:T(8,128)S(1)} fusion(bf16[1,2048,896]{2,1,0:T(8,128)(2,1)} %param.17, bf16[160,4096]{1,0:T(8,128)(2,1)} %all-gather.5.cloned.1.call-done), kind=kOutput, calls=%fused_computation.2 | convolution fusion | flops 587202560 | bytes 4898816 | tf_op jit(solution)/shard_map/dot_general | solution.py:131
  85.8 2.1 %fusion.6 = f32[160,896]{1,0:T(8,128)S(1)} fusion(bf16[1,2048,896]{2,1,0:T(8,128)(2,1)S(1)} %copy-done.1, bf16[160,4096]{1,0:T(8,128)(2,1)} %all-gather.5.cloned.1.call-done), kind=kOutput, calls=%fused_computation.6 | convolution fusion | flops 587202560 | bytes 4898816 | tf_op jit(solution)/shard_map/dot_general | solution.py:132
  88.7 1.0 fusion.18
  90.0 3.5 %fusion.10 = f32[160,896]{1,0:T(8,128)S(1)} fusion(bf16[1,896,2048]{2,1,0:T(8,128)(2,1)} %param.19, bf16[160,4096]{1,0:T(8,128)(2,1)S(1)} %copy-done.6), kind=kOutput, calls=%fused_computation.10 | convolution fusion | flops 587202560 | bytes 4898816 | tf_op jit(solution)/shard_map/dot_general | solution.py:138
  93.6 1.4 fusion
  95.6 1.4 fusion.15
  97.1 4.8 %all_to_all.27 = f32[2,80,2049]{2,1,0:T(8,128)S(1)} all-to-all(f32[2,80,2049]{2,1,0:T(8,128)S(1)} %pad_maximum_fusion), channel_id=1, replica_groups=mesh['section'=8,'expert_0'=4,'expert_1'=4,'dp'=2] {'dp'}, dimensions={0} | all-to-all | bytes 2622720 | tf_op jit(solution)/shard_map/all_to_all | solution.py:64
  102.4 1.1 copy.86
  103.5 6.7 %all-to-all-start.1 = ((f32[16,128,128]{2,1,0:T(8,128)}), f32[16,128,128]{2,1,0:T(8,128)S(1)}, u32[]{:S(2)}, u32[]{:S(2)}) async-start(f32[16,128,128]{2,1,0:T(8,128)} %bitcast.90), calls=%async_computation.1 | async-start | bytes 2097152 | tf_op jit(solution)/shard_map/all_to_all | solution.py:64
  110.5 10.5 %psum.28 = f32[128,4]{0,1:T(4,128)S(1)} all-reduce(f32[128,4]{0,1:T(4,128)S(1)} %broadcast_multiply_fusion), channel_id=1, replica_groups=mesh['section'=8,'expert_0'=4,'expert_1'=4,'dp'=2] {'expert_0'}, use_global_device_ids=true, to_apply=%region_12.13 | all-reduce | flops 512 | bytes 4096 | tf_op jit(solution)/shard_map/psum | solution.py:81
  121.0 11.8 %psum.29 = f32[128,4]{0,1:T(4,128)S(1)} all-reduce(f32[128,4]{0,1:T(4,128)S(1)} %psum.28), channel_id=1, replica_groups=mesh['section'=8,'expert_0'=4,'expert_1'=4,'dp'=2] {'expert_1'}, use_global_device_ids=true, to_apply=%region_13.14 | all-reduce | flops 512 | bytes 4096 | tf_op jit(solution)/shard_map/psum | solution.py:81
  133.4 11.6 %psum.30 = f32[128,1]{0,1:T(1,128)S(1)} all-reduce(f32[128,1]{0,1:T(1,128)S(1)} %bitcast.98), channel_id=1, replica_groups=mesh['section'=8,'expert_0'=4,'expert_1'=4,'dp'=2] {'expert_0'}, use_global_device_ids=true, to_apply=%region_17.18 | all-reduce | flops 128 | bytes 1024 | tf_op jit(solution)/shard_map/psum | solution.py:81
  145.1 10.2 %psum.31 = f32[128]{0:T(128)S(1)} all-reduce(f32[128]{0:T(128)S(1)} %bitcast.101), channel_id=1, replica_groups=mesh['section'=8,'expert_0'=4,'expert_1'=4,'dp'=2] {'expert_1'}, use_global_device_ids=true, to_apply=%region_18.19 | all-reduce | flops 128 | bytes 1024 | tf_op jit(solution)/shard_map/psum | solution.py:81
  155.3 3.4 %collective-permute-start = (bf16[128,128]{0,1:T(8,128)(2,1)S(1)}, bf16[128,128]{0,1:T(8,128)(2,1)S(1)}, u32[]{:S(2)}, u32[]{:S(2)}) collective-permute-start(bf16[128,128]{0,1:T(8,128)(2,1)S(1)} %subtract_convert_fusion), channel_id=1, source_target_pairs={{32,0},{64,32},{96,64},{128,96},{160,128},{192,160},{224,192},{0,2... | collective-permute-start | bytes 98312 | tf_op jit(solution)/shard_map/ppermute | solution.py:88
  (85 shorter events, 11.6 us)
Async XLA Ops:
  7.2 55.1 %copy-start = (bf16[1,2048,4]{1,2,0:T(4,128)(2,1)S(1)}, bf16[1,2048,4]{1,2,0:T(4,128)(2,1)}, u32[]{:S(2)}) copy-start(bf16[1,2048,4]{1,2,0:T(4,128)(2,1)} %param.16) | copy-start | bytes 49156
  7.2 11.7 %copy-start.13 = (s32[1,4]{1,0:T(1,128)S(1)}, s32[1,4]{1,0:T(1,128)}, u32[]{:S(2)}) copy-start(s32[1,4]{1,0:T(1,128)} %param.14) | copy-start | bytes 52
  7.2 12.0 %copy-start.12 = (s32[1,128,2]{1,2,0:T(2,128)S(1)}, s32[1,128,2]{1,2,0:T(2,128)}, u32[]{:S(2)}) copy-start(s32[1,128,2]{1,2,0:T(2,128)} %param.13) | copy-start | bytes 3076
  7.2 53.6 %copy-start.11 = (f32[1,2048]{1,0:T(1,128)S(1)}, f32[1,2048]{1,0:T(1,128)}, u32[]{:S(2)}) copy-start(f32[1,2048]{1,0:T(1,128)} %param.15) | copy-start | bytes 24580
  7.2 52.2 %all-gather.3.cloned.1.call-start = ((), (), s32[]{:S(2)}) async-start(), calls=%async_computation.5 | async-start | bytes 1114112 | tf_op jit(solution)/shard_map/all_gather | solution.py:25
  11.5 53.1 %all-to-all-start.2 = ((f32[16,128,64]{1,2,0:T(8,128)}), f32[16,128,64]{1,2,0:T(8,128)S(1)}, u32[]{:S(2)}, u32[]{:S(2)}) async-start(f32[16,128,64]{1,2,0:T(8,128)} %broadcast_in_dim.10), calls=%async_computation.2 | async-start | bytes 1048576 | tf_op jit(solution)/shard_map/all_to_all | solution.py:36
  18.8 63.6 %all-gather.5.cloned.1.call-start = ((), (), s32[]{:S(2)}) async-start(), calls=%async_computation.6 | async-start | bytes 1966080 | tf_op jit(solution)/shard_map/all_gather | solution.py:25
  60.8 2.5 %copy-start.3 = (bf16[256,2048]{0,1:T(8,128)(2,1)S(1)}, bf16[256,2048]{0,1:T(8,128)(2,1)}, u32[]{:S(2)}) copy-start(bf16[256,2048]{0,1:T(8,128)(2,1)} %all-gather.3.cloned.1.call-done) | copy-start | bytes 3145732
  63.3 1.3 copy-start.10
  64.6 13.3 %copy-start.9 = (bf16[1,128,128]{2,1,0:T(8,128)(2,1)S(1)}, bf16[1,128,128]{2,1,0:T(8,128)(2,1)}, u32[]{:S(2)}) copy-start(bf16[1,128,128]{2,1,0:T(8,128)(2,1)} %param.12) | copy-start | bytes 98308
  65.4 12.5 %all-to-all-start.3 = ((bf16[16,128,64]{1,2,0:T(8,128)(2,1)}), bf16[16,128,64]{1,2,0:T(8,128)(2,1)S(1)}, u32[]{:S(2)}, u32[]{:S(2)}) async-start(bf16[16,128,64]{1,2,0:T(8,128)(2,1)} %broadcast_in_dim.13), calls=%async_computation.3 | async-start | bytes 524288 | tf_op jit(solution)/shard_map/all_to_all | solution.py:36
  82.4 3.3 %copy-start.1 = (bf16[1,2048,896]{2,1,0:T(8,128)(2,1)S(1)}, bf16[1,2048,896]{2,1,0:T(8,128)(2,1)}, u32[]{:S(2)}) copy-start(bf16[1,2048,896]{2,1,0:T(8,128)(2,1)} %param.18) | copy-start | bytes 11010052
  82.4 6.3 %copy-start.6 = (bf16[160,4096]{1,0:T(8,128)(2,1)S(1)}, bf16[160,4096]{1,0:T(8,128)(2,1)}, u32[]{:S(2)}) copy-start(bf16[160,4096]{1,0:T(8,128)(2,1)} %all-gather.5.cloned.1.call-done) | copy-start | bytes 3932164
  85.8 3.0 %copy-start.4 = (bf16[1,896,2048]{2,1,0:T(8,128)(2,1)S(1)}, bf16[1,896,2048]{2,1,0:T(8,128)(2,1)}, u32[]{:S(2)}) copy-start(bf16[1,896,2048]{2,1,0:T(8,128)(2,1)} %param.19) | copy-start | bytes 11010052
  87.9 0.8 copy-start.7
  90.0 3.6 %copy-start.5 = (bf16[1,2048,896]{2,1,0:T(8,128)(2,1)S(1)}, bf16[1,2048,896]{2,1,0:T(8,128)(2,1)}, u32[]{:S(2)}) copy-start(bf16[1,2048,896]{2,1,0:T(8,128)(2,1)} %param.17) | copy-start | bytes 11010052
  90.0 3.6 %copy-start.8 = (f32[160,896]{1,0:T(8,128)S(1)}, f32[160,896]{1,0:T(8,128)}, u32[]{:S(2)}) copy-start(f32[160,896]{1,0:T(8,128)} %copy-done.7) | copy-start | bytes 1720324
  93.6 2.0 %copy-start.2 = (bf16[1,2048,896]{2,1,0:T(8,128)(2,1)S(1)}, bf16[1,2048,896]{2,1,0:T(8,128)(2,1)}, u32[]{:S(2)}) copy-start(bf16[1,2048,896]{2,1,0:T(8,128)(2,1)} %param.18) | copy-start | bytes 11010052
  103.5 29.5 %all-to-all-start.1 = ((f32[16,128,128]{2,1,0:T(8,128)}), f32[16,128,128]{2,1,0:T(8,128)S(1)}, u32[]{:S(2)}, u32[]{:S(2)}) async-start(f32[16,128,128]{2,1,0:T(8,128)} %bitcast.90), calls=%async_computation.1 | async-start | bytes 2097152 | tf_op jit(solution)/shard_map/all_to_all | solution.py:64
  155.3 5.0 %collective-permute-start = (bf16[128,128]{0,1:T(8,128)(2,1)S(1)}, bf16[128,128]{0,1:T(8,128)(2,1)S(1)}, u32[]{:S(2)}, u32[]{:S(2)}) collective-permute-start(bf16[128,128]{0,1:T(8,128)(2,1)S(1)} %subtract_convert_fusion), channel_id=1, source_target_pairs={{32,0},{64,32},{96,64},{128,96},{160,128},{192,160},{224,192},{0,2... | collective-permute-start | bytes 98312 | tf_op jit(solution)/shard_map/ppermute | solution.py:88
Sparse Core Ops, SparseCore 0:
  10.5 48.9 all-gather.2
  64.7 15.6 all-gather.4
where the time goes:
time: 169 us; the launch traced here: 168 us
  blocking collectives  52.7 us (31%)
  waiting for transfers between devices  45.8 us (27%)
  starting transfers between devices  24.4 us (14%)
  matrix products  15.9 us (9%)
  between operations  14.4 us (9%)
  local copies, waits for them, and re-layouts  8.89 us (5%)
  other arithmetic  5.75 us (3%)
    psum x4, blocking collectives, over_axes(): x = lax.psum(x, axis)  44.1 us
    all_gather x2, waiting for transfers between devices, in_one_piece(): lax.all_gather(both, axis, axis=dim, tiled=True)  40.3 us
    all_to_all x2, starting transfers between devices, from_everyone(): lax.all_to_all(jnp.broadcast_to(x[None], (devices, *x.shape)), axis, 0, 0...  14.3 us
    all_to_all x1, starting transfers between devices, sent_and_summed(): lax.all_to_all(blocks, axis, split_axis=0, concat_axis=0, tiled=True)  6.65 us
    all_to_all x2, waiting for transfers between devices, from_everyone(): lax.all_to_all(jnp.broadcast_to(x[None], (devices, *x.shape)), axis, 0, 0...  5.27 us
    all_to_all x1, blocking collectives, sent_and_summed(): lax.all_to_all(blocks, axis, split_axis=0, concat_axis=0, tiled=True)  4.83 us
    unnamed x32, local copies, waits for them, and re-layouts  4.79 us
    all_to_all x1, blocking collectives, from_everyone(): lax.all_to_all(jnp.broadcast_to(x[None], (devices, *x.shape)), axis, 0, 0...  3.84 us
  transfers between devices with their start and end apart: 6, of which 3 were waited for; matrix products, arithmetic and copies ran while one was open for 6% of the time, Pallas kernels for 0%

commit v1 on v0

v1 whole, which is shorter than its diff:
```python
import jax
import jax.numpy as jnp
from jax import lax
from jax.experimental import pallas as pl
from jax.experimental.pallas import tpu as pltpu
from jax.sharding import Mesh
from jax.sharding import PartitionSpec as P

MODEL_WIDTH = 2048
EXPERTS = 4
RANK = 16
JOBS = 4
CAP = 80
TOK = 128
COLS = 128
GROUPS = 16
STATS = 48
SEND = 2 * CAP + STATS
BACK = CAP + 16
HIDDEN = 896
EXPERT = ("expert_0", "expert_1")
EXPERT_DP = ("expert_0", "expert_1", "dp")
EPS = 1e-05
ADAPTER_SCALE = 0.5
F32 = jnp.float32
BF16 = jnp.bfloat16


def dot(a, b, ca, cb):
    return lax.dot_general(a, b, (((ca,), (cb,)), ((), ())), preferred_element_type=F32)


def high_low(v):
    high = v.astype(BF16)
    return high, (v - high.astype(F32)).astype(BF16)


def slot_places(routes):
    lanes = lax.broadcasted_iota(jnp.int32, (TOK, 128), 1)
    first, second = routes[:, 0:1], routes[:, 1:2]
    member = ((lanes == first) | (lanes == second)).astype(BF16)
    earlier = (
        lax.broadcasted_iota(jnp.int32, (TOK, TOK), 1)
        < lax.broadcasted_iota(jnp.int32, (TOK, TOK), 0)
    ).astype(BF16)
    rank = dot(earlier, member, 1, 0)
    places = []
    for chosen in (first, second):
        at = jnp.sum(jnp.where(lanes == chosen, rank, 0.0), axis=1, keepdims=True)
        places.append(chosen * 128 + at.astype(jnp.int32))
    return places


def owner_mask(scalars, offset, count):
    token = offset + lax.broadcasted_iota(jnp.int32, (JOBS * RANK, count), 1)
    job = lax.broadcasted_iota(jnp.int32, (JOBS * RANK, count), 0) // RANK
    owner = jnp.zeros((JOBS * RANK, count), jnp.int32)
    end = jnp.int32(0)
    for j in range(JOBS):
        end = end + scalars[2 + j]
        owner = owner + (token >= end).astype(jnp.int32)
    return owner == job


def prepare_kernel(scalars, x_ref, g_ref, routes_ref, gain_ref, router_ref, down_ref, up_ref, out_ref):
    x = x_ref[...]
    g = g_ref[...]
    first, second = slot_places(routes_ref[...])
    for e in range(EXPERTS):
        lanes = e * 128 + lax.broadcasted_iota(jnp.int32, (TOK, 128), 1)
        hit = ((lanes == first) | (lanes == second)).astype(F32)
        pick = hit.T[:CAP].astype(BF16)
        xs = dot(pick, x, 1, 0).astype(BF16)
        gs = dot(pick, g, 1, 0).astype(BF16)
        for k in range(GROUPS // EXPERTS):
            out_ref[e * 4 + k, 0:CAP, :] = xs
            out_ref[e * 4 + k, CAP : 2 * CAP, :] = gs
    xf = x.astype(F32)
    xg = (xf * gain_ref[...]).astype(BF16)
    mask = owner_mask(scalars, scalars[1] * TOK, TOK)
    low = jnp.where(mask, dot(down_ref[...].astype(F32).T.astype(BF16), xg, 1, 1), 0.0)
    dlow = jnp.where(mask, dot(up_ref[...], g, 1, 1), 0.0)
    low16 = low[0:16] + low[16:32] + low[32:48] + low[48:64]
    dlow16 = dlow[0:16] + dlow[16:32] + dlow[32:48] + dlow[48:64]
    wide = jnp.concatenate([router_ref[...].astype(F32), jnp.zeros((COLS, 124), F32)], axis=1)
    logits = dot(wide.T[:8].astype(BF16), xg, 1, 1)
    square = xf * xf
    squares = jnp.sum(square.T, axis=0, keepdims=True)
    row = lax.broadcasted_iota(jnp.int32, (8, TOK), 0)
    small = jnp.where(row == 4, squares, logits)
    high = small.astype(BF16).astype(F32)
    stats = jnp.concatenate([low16, dlow16, high, small - high], axis=0).astype(BF16)
    for k in range(GROUPS):
        out_ref[k, 2 * CAP :, :] = stats


def expert_kernel(own_ref, other_ref, gain_ref, wg_ref, wu_ref, wd_ref, own_out, other_out, x_s, g_s, da_s, db_s):
    for d, ref in enumerate((own_ref, other_ref)):
        rows = slice(d * CAP, (d + 1) * CAP)
        total = jnp.zeros((CAP, 128), F32)
        for c in range(GROUPS):
            v = ref[c, 0:CAP, :].astype(F32)
            total = total + v * v
        scale = lax.rsqrt(jnp.sum(total, axis=1, keepdims=True) / MODEL_WIDTH + EPS)
        for c in range(GROUPS):
            cols = slice(c * 128, (c + 1) * 128)
            x_s[rows, cols] = (ref[c, 0:CAP, :].astype(F32) * scale * gain_ref[:, cols]).astype(BF16)
            g_s[rows, cols] = ref[c, CAP : 2 * CAP, :]
    gate_terms = jnp.zeros((2 * CAP, 128), F32)
    stat_terms = jnp.zeros((2 * CAP, 128), F32)
    for lower in range(0, HIDDEN, 256):
        size = min(256, HIDDEN - lower)
        cols = slice(lower, lower + size)
        a = dot(x_s[...], wg_ref[:, cols], 1, 0)
        b = dot(x_s[...], wu_ref[:, cols], 1, 0)
        back = dot(g_s[...], wd_ref[cols, :], 1, 1)
        sig = jax.nn.sigmoid(a)
        act = a * sig
        da = back * b * sig * (1.0 + a * (1.0 - sig))
        db = back * act
        gate = act * b * back
        stat = da * a + db * b
        for k in range(0, size, 128):
            gate_terms = gate_terms + gate[:, k : k + 128]
            stat_terms = stat_terms + stat[:, k : k + 128]
        da_s[:, cols] = da.astype(BF16)
        db_s[:, cols] = db.astype(BF16)
    lane = lax.broadcasted_iota(jnp.int32, (2 * CAP, 128), 1)
    dgate = jnp.sum(gate_terms, axis=1, keepdims=True)
    dstat = jnp.sum(stat_terms, axis=1, keepdims=True)
    table = jnp.where(lane == 0, dgate, jnp.where(lane == 1, dstat, 0.0))
    row = lax.broadcasted_iota(jnp.int32, (8, 128), 0)
    for d, out in enumerate((own_out, other_out)):
        part = jnp.concatenate([table[d * CAP : (d + 1) * CAP], jnp.zeros((128 - CAP, 128), F32)], axis=0)
        lines = part.T[0:8]
        high = lines.astype(BF16).astype(F32)
        packed = jnp.where(row < 2, high, 0.0) + jnp.where((row >= 2) & (row < 4), jnp.roll(lines - high, 2, 0), 0.0)
        packed = jnp.concatenate([packed, jnp.zeros((8, 128), F32)] if d == 0 else [jnp.zeros((8, 128), F32), packed], axis=0)
        for c in range(GROUPS):
            out[c, CAP:BACK, :] = packed.astype(out.dtype)
    for lower in range(0, MODEL_WIDTH, 256):
        rows = slice(lower, lower + 256)
        dn = dot(da_s[...], wg_ref[rows, :], 1, 1) + dot(db_s[...], wu_ref[rows, :], 1, 1)
        for k in range(2):
            c = lower // 128 + k
            own_out[c, 0:CAP, :] = dn[0:CAP, k * 128 : (k + 1) * 128]
            other_out[c, 0:CAP, :] = dn[CAP:, k * 128 : (k + 1) * 128].astype(BF16)


def stats_kernel(
    scalars, own_ref, other_ref, x_ref, g_ref, xo_ref, go_ref, gain_ref, down_ref,
    grad_down_ref, grad_up_ref, side_ref, base_ref, sb_ref
):
    grad_down = jnp.zeros((JOBS * RANK, COLS), F32)
    grad_up = jnp.zeros((JOBS * RANK, COLS), F32)
    me = scalars[1]
    for d, (ref, xr, gr) in enumerate(((own_ref, x_ref, g_ref), (other_ref, xo_ref, go_ref))):
        total = ref[0, 2 * CAP :, :].astype(F32)
        for c in range(1, GROUPS):
            total = total + ref[c, 2 * CAP :, :].astype(F32)
        small = total[32:40] + total[40:48]
        scale = lax.rsqrt(small[4:5] / MODEL_WIDTH + EPS)
        block = me if d == 0 else 1 - me
        mask = owner_mask(scalars, block * TOK, TOK)
        low16 = total[0:16]
        dlow16 = ADAPTER_SCALE * total[16:32]
        low = jnp.where(mask, jnp.concatenate([low16 * scale] * JOBS, axis=0), 0.0).astype(BF16)
        dlow = jnp.where(mask, jnp.concatenate([dlow16] * JOBS, axis=0), 0.0).astype(BF16)
        row = lax.broadcasted_iota(jnp.int32, (8, TOK), 0)
        adapter_stat = jnp.sum(dlow16.astype(BF16).astype(F32) * low16, axis=0, keepdims=True)
        lines = jnp.where(row == 4, scale, jnp.where(row == 5, adapter_stat, small))
        side = jnp.concatenate([lines, jnp.zeros((120, TOK), F32)], axis=0).T
        xf = xr[...].astype(F32)
        scale_col = side[:, 4:5]
        normed = (xf * scale_col * gain_ref[...]).astype(BF16)
        grad_down = grad_down + dot(dlow, normed, 1, 0)
        grad_up = grad_up + dot(low, gr[...], 1, 0)
        if d == 0:
            side_ref[...] = side
            adapter = dot(down_ref[...], dlow, 1, 0).T
            base_ref[...] = gr[...].astype(F32) + scale_col * adapter * gain_ref[...]
            sb_ref[...] = xf * scale_col * scale_col * scale_col / MODEL_WIDTH
    wide = jnp.concatenate([grad_down, jnp.zeros((64, COLS), F32)], axis=0)
    grad_down_ref[...] = wide.T[:, 0 : JOBS * RANK]
    grad_up_ref[...] = ADAPTER_SCALE * grad_up


def finish_kernel(scalars, in_ref, routes_ref, gain_ref, router_ref, side_ref, base_ref, sb_ref, out_ref):
    routes = routes_ref[...]
    first, second = slot_places(routes)
    side = side_ref[...]
    lane = lax.broadcasted_iota(jnp.int32, (TOK, 128), 1)

    def chosen(k):
        return jnp.sum(jnp.where(lane == routes[:, k : k + 1], side, 0.0), axis=1, keepdims=True)

    scale = side[:, 4:5]
    raw = chosen(0) - chosen(1)
    upper = jax.nn.sigmoid(raw * scale)
    lower = 1.0 - upper
    rows1 = jnp.zeros((TOK, COLS), F32)
    rows2 = jnp.zeros((TOK, COLS), F32)
    gate1 = jnp.zeros((TOK, 128), F32)
    gate2 = jnp.zeros((TOK, 128), F32)
    stat1 = jnp.zeros((TOK, 128), F32)
    stat2 = jnp.zeros((TOK, 128), F32)
    for e in range(EXPERTS):
        total = in_ref[4 * e].astype(F32)
        for k in range(1, 4):
            total = total + in_ref[4 * e + k].astype(F32)
        lines = total[CAP : CAP + 8] + total[CAP + 8 : CAP + 16]
        dgate = lines[0:1] + lines[2:3]
        dstat = lines[1:2] + lines[3:4]
        hit1 = lane + e * 128 == first
        hit2 = lane + e * 128 == second
        gate1 = gate1 + jnp.where(hit1, dgate, 0.0)
        gate2 = gate2 + jnp.where(hit2, dgate, 0.0)
        stat1 = stat1 + jnp.where(hit1, dstat, 0.0)
        stat2 = stat2 + jnp.where(hit2, dstat, 0.0)
        high, low = high_low(total[0:CAP])
        one = hit1[:, 0:CAP].astype(BF16)
        two = hit2[:, 0:CAP].astype(BF16)
        rows1 = rows1 + dot(one, high, 1, 0) + dot(one, low, 1, 0)
        rows2 = rows2 + dot(two, high, 1, 0) + dot(two, low, 1, 0)
    spread = jnp.sum(gate1 - gate2, axis=1, keepdims=True)
    delta = spread * upper * lower
    expert_stat = upper * jnp.sum(stat1, axis=1, keepdims=True) + lower * jnp.sum(stat2, axis=1, keepdims=True)
    stat = expert_stat / scale + side[:, 5:6] + delta * raw
    wide = jnp.concatenate([router_ref[...].astype(F32), jnp.zeros((COLS, 124), F32)], axis=1).T
    routed = jnp.zeros((TOK, COLS), F32)
    for e in range(EXPERTS):
        sign = (routes[:, 0:1] == e).astype(F32) - (routes[:, 1:2] == e).astype(F32)
        routed = routed + sign * wide[e : e + 1]
    dnormed = upper * rows1 + lower * rows2 + delta * routed
    result = base_ref[...] + scale * dnormed * gain_ref[...] - sb_ref[...] * stat
    out_ref[...] = result.astype(BF16)


def whole(shape):
    return pl.BlockSpec(shape, lambda i, s: (0,) * len(shape))


GAIN_BLOCK = pl.BlockSpec((1, COLS), lambda i, s: (0, s[0]))
ROUTER_BLOCK = pl.BlockSpec((COLS, EXPERTS), lambda i, s: (s[0], 0))


def call(kernel, scalars, in_specs, out_specs, out_shape, args, scratch=()):
    return pl.pallas_call(
        kernel,
        grid_spec=pltpu.PrefetchScalarGridSpec(
            num_scalar_prefetch=1, grid=(1,), in_specs=in_specs, out_specs=out_specs, scratch_shapes=scratch
        ),
        out_shape=out_shape,
    )(scalars, *args)


def shards(stash, cotangent, routes, lengths, gains, router, wg, wu, wd, down, up):
    x, g, routes, router = stash[0], cotangent[0], routes[0], router[0]
    wg, wu, wd, down, up = wg[0], wu[0], wd[0], down[0], up[0]
    shape = jax.ShapeDtypeStruct
    scalars = jnp.concatenate(
        [
            jnp.stack([lax.axis_index(EXPERT), lax.axis_index("dp")]).astype(jnp.int32),
            lengths[0],
        ]
    )
    swap = [(0, 1), (1, 0)]
    xo = lax.ppermute(x, "dp", swap)
    go = lax.ppermute(g, "dp", swap)
    sent = call(
        prepare_kernel,
        scalars,
        [
            whole((TOK, COLS)), whole((TOK, COLS)), whole((TOK, 2)), GAIN_BLOCK, ROUTER_BLOCK,
            whole((COLS, JOBS * RANK)), whole((JOBS * RANK, COLS)),
        ],
        whole((GROUPS, SEND, 128)),
        shape((GROUPS, SEND, 128), BF16),
        (x, g, routes, gains, router, down, up),
    )
    own = lax.all_to_all(sent, EXPERT, 0, 0, tiled=True)
    other = lax.ppermute(own, "dp", swap)
    vmem = pl.BlockSpec(memory_space=pltpu.VMEM)
    own_part, other_part = pl.pallas_call(
        expert_kernel,
        in_specs=[vmem] * 6,
        out_specs=(vmem, vmem),
        out_shape=(shape((GROUPS, BACK, 128), F32), shape((GROUPS, BACK, 128), BF16)),
        scratch_shapes=[
            pltpu.VMEM((2 * CAP, MODEL_WIDTH), BF16),
            pltpu.VMEM((2 * CAP, MODEL_WIDTH), BF16),
            pltpu.VMEM((2 * CAP, HIDDEN), BF16),
            pltpu.VMEM((2 * CAP, HIDDEN), BF16),
        ],
        compiler_params=pltpu.CompilerParams(vmem_limit_bytes=40 * 1024 * 1024),
    )(own, other, gains, wg, wu, wd)
    arrived = lax.ppermute(other_part, "dp", swap)
    parts = (own_part + arrived.astype(F32)).astype(BF16)
    back = lax.all_to_all(parts, EXPERT, 0, 0, tiled=True)
    grad_down, grad_up, side, base, sb = call(
        stats_kernel,
        scalars,
        [
            whole((GROUPS, SEND, 128)), whole((GROUPS, SEND, 128)), whole((TOK, COLS)), whole((TOK, COLS)),
            whole((TOK, COLS)), whole((TOK, COLS)), GAIN_BLOCK, whole((COLS, JOBS * RANK)),
        ],
        (whole((COLS, JOBS * RANK)), whole((JOBS * RANK, COLS)), whole((TOK, 128)), whole((TOK, COLS)), whole((TOK, COLS))),
        (
            shape((COLS, JOBS * RANK), F32), shape((JOBS * RANK, COLS), F32), shape((TOK, 128), F32),
            shape((TOK, COLS), F32), shape((TOK, COLS), F32),
        ),
        (own, other, x, g, xo, go, gains, down),
    )
    result = call(
        finish_kernel,
        scalars,
        [
            whole((GROUPS, BACK, 128)), whole((TOK, 2)), GAIN_BLOCK, ROUTER_BLOCK,
            whole((TOK, 128)), whole((TOK, COLS)), whole((TOK, COLS)),
        ],
        whole((TOK, COLS)),
        shape((TOK, COLS), BF16),
        (back, routes, gains, router, side, base, sb),
    )
    count = lax.axis_size("section")
    handed = lax.ppermute(result, "section", [(i, (i - 1) % count) for i in range(count)])
    return handed[None], grad_down[None], grad_up[None]


def solution(mesh):
    finer = Mesh(
        mesh.devices.reshape(mesh.shape["section"], 4, 4, mesh.shape["dp"]),
        ("section", "expert_0", "expert_1", "dp"),
    )
    in_specs = (
        P("section", "dp", EXPERT),
        P("section", "dp", EXPERT),
        P("section", "dp", None),
        P("section", None),
        P("section", None),
        P("section", None, None),
        P("section", None, EXPERT_DP),
        P("section", None, EXPERT_DP),
        P("section", EXPERT_DP, None),
        P("section", EXPERT, None),
        P("section", None, EXPERT),
    )
    out_specs = (P("section", "dp", EXPERT), P("section", EXPERT, None), P("section", None, EXPERT))
    return jax.shard_map(shards, mesh=finer, in_specs=in_specs, out_specs=out_specs, check_vma=False)
```

time: 169 us -> 75.2 us (0.44)
  the two profiles are of different devices: /device:TPU:10 before, /device:TPU:1 now
where the time goes in v1:
time: 75.2 us; the launch traced here: 74.5 us
  blocking collectives  21.8 us (29%)
  Pallas kernels  15 us (20%)
  local copies, waits for them, and re-layouts  14.8 us (20%)
  starting transfers between devices  12 us (16%)
  waiting for transfers between devices  8.14 us (11%)
  other arithmetic  2.11 us (3%)
    all_to_all x1, blocking collectives, shards(): own = lax.all_to_all(sent, EXPERT, 0, 0, tiled=True)  21.8 us
    unnamed x27, local copies, waits for them, and re-layouts  14.8 us
    pallas_call x3, Pallas kernels, call(): pl.pallas_call(kernel, grid_spec=pltpu.PrefetchScalarGridSpec(num_scalar_...  9.86 us
    ppermute x1, starting transfers between devices, shards(): lax.ppermute(result, 'section', [(i, (i - 1) % count) for i in range(coun...  5.57 us
    pallas_call x1, Pallas kernels, shards(): pl.pallas_call(expert_kernel, in_specs=[vmem] * 6, out_specs=(vmem, vmem)...  5.17 us
    all_to_all x1, waiting for transfers between devices, shards(): back = lax.all_to_all(parts, EXPERT, 0, 0, tiled=True)  3.71 us
    all_to_all x1, starting transfers between devices, shards(): back = lax.all_to_all(parts, EXPERT, 0, 0, tiled=True)  3.55 us
    ppermute x1, waiting for transfers between devices, shards(): other = lax.ppermute(own, 'dp', swap)  2.01 us
  transfers between devices with their start and end apart: 6, of which 5 were waited for; matrix products, arithmetic and copies ran while one was open for 2% of the time, Pallas kernels for 4%

profile of v1, /device:TPU:1, one launch (start us, length us, event | category | flops | bytes accessed | tf_op | source)
XLA Modules:
  0.0 74.5 jit_solution(16558445923721838742)
XLA Ops:
  0.6 1.4 %copy.16 = bf16[1,128,64]{2,1,0:T(8,128)(2,1)} copy(bf16[1,128,64]{1,2,0:T(8,128)(2,1)} %param.20) | data formatting | bytes 32768 | tf_op args[9]
  2.1 1.4 %copy.14 = s32[1,128,2]{2,1,0:T(8,128)} copy(s32[1,128,2]{1,2,0:T(2,128)} %param.13) | data formatting | bytes 2048 | tf_op args[2]
  3.5 1.8 %copy.15 = bf16[1,2048,4]{2,1,0:T(8,128)(2,1)} copy(bf16[1,2048,4]{1,2,0:T(4,128)(2,1)} %param.16) | data formatting | bytes 32768 | tf_op args[5]
  5.2 1.3 %pad_add_fusion.scalars = s32[6]{0:T(128)} fusion(s32[4]{0:T(128)} %bitcast.33, s32[1]{0:T(128)} %bitcast.1, s32[1]{0:T(128)} %bitcast), kind=kLoop, calls=%fused_computation.1 | loop fusion | flops 12 | bytes 48 | tf_op jit(solution)/shard_map/concatenate | solution.py:261
  6.5 3.3 %shard_map.130 = bf16[16,208,128]{2,1,0:T(8,128)(2,1)} custom-call(s32[6]{0:T(128)} %pad_add_fusion.scalars, bf16[128,128]{1,0:T(8,128)(2,1)} %bitcast.24, bf16[128,128]{1,0:T(8,128)(2,1)} %bitcast.27, s32[128,2]{1,0:T(8,128)} %bitcast.20, f32[1,2048]{1,0:T(1,128)} %gain_ref.7, bf16[2048,4]{1,0:T(8,128)(2,1)} %bitcast.18, bf16[128,64]{1,0:T(8,128)(2,1)} %bitcast.22, ...), custom_call_target="tpu_custom_call" | custom-call | tf_op jit(solution)/shard_map/pallas_call | solution.py:248
  9.8 21.8 %all_to_all.10.own_ref = bf16[16,208,128]{2,1,0:T(8,128)(2,1)S(1)} all-to-all(bf16[16,208,128]{2,1,0:T(8,128)(2,1)} %shard_map.130), channel_id=1, replica_groups=mesh['section'=8,'expert_0'=4,'expert_1'=4,'dp'=2] {'expert_0','expert_1'}, dimensions={0} | all-to-all | bytes 1703936 | tf_op jit(solution)/shard_map/all_to_all | solution.py:281
  31.6 1.8 %collective-permute-start = (bf16[16,208,128]{2,1,0:T(8,128)(2,1)S(1)}, bf16[16,208,128]{2,1,0:T(8,128)(2,1)S(1)}, u32[]{:S(2)}, u32[]{:S(2)}) collective-permute-start(bf16[16,208,128]{2,1,0:T(8,128)(2,1)S(1)} %all_to_all.10.own_ref), channel_id=1, source_target_pairs={{0,1},{1,0},{2,3},{3,2},{4,5},{5,4},{6,7},{7,6},{8,9},{9,8},{10,11... | collective-permute-start | bytes 2555912 | tf_op jit(solution)/shard_map/ppermute | solution.py:282
  33.4 2.0 %collective-permute-done.other_ref = bf16[16,208,128]{2,1,0:T(8,128)(2,1)S(1)} collective-permute-done((bf16[16,208,128]{2,1,0:T(8,128)(2,1)S(1)}, bf16[16,208,128]{2,1,0:T(8,128)(2,1)S(1)}, u32[]{:S(2)}, u32[]{:S(2)}) %collective-permute-start) | collective-permute-done | bytes 852000 | tf_op jit(solution)/shard_map/ppermute | solution.py:282
  35.4 2.3 %copy-done.1 = bf16[1,2048,896]{2,1,0:T(8,128)(2,1)S(1)} copy-done((bf16[1,2048,896]{2,1,0:T(8,128)(2,1)S(1)}, bf16[1,2048,896]{2,1,0:T(8,128)(2,1)}, u32[]{:S(2)}) %copy-start.1) | copy-done | bytes 3670040
  37.7 2.0 %copy-done.2 = bf16[1,2048,896]{2,1,0:T(8,128)(2,1)S(1)} copy-done((bf16[1,2048,896]{2,1,0:T(8,128)(2,1)S(1)}, bf16[1,2048,896]{2,1,0:T(8,128)(2,1)}, u32[]{:S(2)}) %copy-start.2) | copy-done | bytes 3670040
  39.8 2.0 %copy-done.3 = bf16[1,896,2048]{2,1,0:T(8,128)(2,1)S(1)} copy-done((bf16[1,896,2048]{2,1,0:T(8,128)(2,1)S(1)}, bf16[1,896,2048]{2,1,0:T(8,128)(2,1)}, u32[]{:S(2)}) %copy-start.3) | copy-done | bytes 3670040
  41.8 5.2 %shard_map.131 = (f32[16,96,128]{2,1,0:T(8,128)S(1)}, bf16[16,96,128]{2,1,0:T(8,128)(2,1)S(1)}) custom-call(bf16[16,208,128]{2,1,0:T(8,128)(2,1)S(1)} %all_to_all.10.own_ref, bf16[16,208,128]{2,1,0:T(8,128)(2,1)S(1)} %collective-permute-done.other_ref, f32[1,2048]{1,0:T(1,128)S(1)} %copy-done.5, bf16[2048,896]{1,0:T(8,128)(2,1)S(1)} %bitcast.15, ...), custom_call_target="tpu_custom_call" | custom-call | tf_op jit(solution)/shard_map/pallas_call | solution.py:284
  47.5 1.4 %collective-permute-done.1 = bf16[16,96,128]{2,1,0:T(8,128)(2,1)S(1)} collective-permute-done((bf16[16,96,128]{2,1,0:T(8,128)(2,1)S(1)}, bf16[16,96,128]{2,1,0:T(8,128)(2,1)S(1)}, u32[]{:S(2)}, u32[]{:S(2)}) %collective-permute-start.1) | collective-permute-done | bytes 393248 | tf_op jit(solution)/shard_map/ppermute | solution.py:297
  48.8 0.8 %add_convert_fusion = bf16[16,96,128]{2,1,0:T(8,128)(2,1)} fusion(f32[16,96,128]{2,1,0:T(8,128)S(1)} %get-tuple-element.10, bf16[16,96,128]{2,1,0:T(8,128)(2,1)S(1)} %collective-permute-done.1), kind=kLoop, calls=%fused_computation | loop fusion | flops 589824 | bytes 1572864 | tf_op jit(solution)/shard_map/convert_element_type | solution.py:298
  49.6 3.6 %all-to-all-start.1 = ((bf16[16,96,128]{2,1,0:T(8,128)(2,1)}), bf16[16,96,128]{2,1,0:T(8,128)(2,1)S(1)}, u32[]{:S(2)}, u32[]{:S(2)}) async-start(bf16[16,96,128]{2,1,0:T(8,128)(2,1)} %add_convert_fusion), calls=%async_computation.1 | async-start | bytes 786432 | tf_op jit(solution)/shard_map/all_to_all | solution.py:299
  53.8 0.7 collective-permute-done.2.xo_ref
  55.2 0.6 copy-done.10
  55.8 3.3 %shard_map.132 = (f32[128,64]{1,0:T(8,128)}, f32[64,128]{1,0:T(8,128)}, f32[128,128]{1,0:T(8,128)}, f32[128,128]{1,0:T(8,128)}, f32[128,128]{1,0:T(8,128)}) custom-call(s32[6]{0:T(128)} %pad_add_fusion.scalars, bf16[16,208,128]{2,1,0:T(8,128)(2,1)} %copy-done, bf16[16,208,128]{2,1,0:T(8,128)(2,1)} %copy-done.4, bf16[128,128]{1,0:T(8,128)(2,1)} %bitcast.25, ...), custom_call_target="tpu_custom_call" | custom-call | tf_op jit(solution)/shard_map/pallas_call | solution.py:248
  59.0 3.7 %all-to-all-done.1.in_ref = bf16[16,96,128]{2,1,0:T(8,128)(2,1)S(1)} async-done(((bf16[16,96,128]{2,1,0:T(8,128)(2,1)}), bf16[16,96,128]{2,1,0:T(8,128)(2,1)S(1)}, u32[]{:S(2)}, u32[]{:S(2)}) %all-to-all-start.1) | async-done | bytes 393248 | tf_op jit(solution)/shard_map/all_to_all | solution.py:299
  62.7 0.7 copy-done.6
  63.5 3.4 %shard_map.133 = bf16[128,128]{1,0:T(8,128)(2,1)} custom-call(s32[6]{0:T(128)} %pad_add_fusion.scalars, bf16[16,96,128]{2,1,0:T(8,128)(2,1)} %copy-done.6, s32[128,2]{1,0:T(8,128)} %bitcast.21, f32[1,2048]{1,0:T(1,128)} %gain_ref.7, bf16[2048,4]{1,0:T(8,128)(2,1)} %bitcast.19, f32[128,128]{1,0:T(8,128)} %get-tuple-element.12.side_ref, ...), custom_call_target="tpu_custom_call" | custom-call | tf_op jit(solution)/shard_map/pallas_call | solution.py:248
  66.8 5.6 %collective-permute-start.4 = (bf16[128,128]{1,0:T(8,128)(2,1)}, bf16[128,128]{1,0:T(8,128)(2,1)S(1)}, u32[]{:S(2)}, u32[]{:S(2)}) collective-permute-start(bf16[128,128]{1,0:T(8,128)(2,1)} %shard_map.133), channel_id=1, source_target_pairs={{0,224},{32,0},{64,32},{96,64},{128,96},{160,128},{192,160},{224,1... | collective-permute-start | bytes 98312 | tf_op jit(solution)/shard_map/ppermute | solution.py:326
  72.4 1.5 %copy.17 = f32[1,128,64]{1,2,0:T(8,128)} copy(f32[1,128,64]{2,1,0:T(8,128)} %bitcast.30) | data formatting | bytes 65536
  73.9 0.6 copy.19
  (22 shorter events, 1.7 us)
Async XLA Ops:
  0.6 34.8 %copy-start.5 = (f32[1,2048]{1,0:T(1,128)S(1)}, f32[1,2048]{1,0:T(1,128)}, u32[]{:S(2)}) copy-start(f32[1,2048]{1,0:T(1,128)} %gain_ref.7) | copy-start | bytes 24580
  31.6 15.4 %copy-start = (bf16[16,208,128]{2,1,0:T(8,128)(2,1)}, bf16[16,208,128]{2,1,0:T(8,128)(2,1)S(1)}, u32[]{:S(2)}) copy-start(bf16[16,208,128]{2,1,0:T(8,128)(2,1)S(1)} %all_to_all.10.own_ref) | copy-start | bytes 2555908
  31.6 3.8 %collective-permute-start = (bf16[16,208,128]{2,1,0:T(8,128)(2,1)S(1)}, bf16[16,208,128]{2,1,0:T(8,128)(2,1)S(1)}, u32[]{:S(2)}, u32[]{:S(2)}) collective-permute-start(bf16[16,208,128]{2,1,0:T(8,128)(2,1)S(1)} %all_to_all.10.own_ref), channel_id=1, source_target_pairs={{0,1},{1,0},{2,3},{3,2},{4,5},{5,4},{6,7},{7,6},{8,9},{9,8},{10,11... | collective-permute-start | bytes 2555912 | tf_op jit(solution)/shard_map/ppermute | solution.py:282
  35.4 11.6 %copy-start.4 = (bf16[16,208,128]{2,1,0:T(8,128)(2,1)}, bf16[16,208,128]{2,1,0:T(8,128)(2,1)S(1)}, u32[]{:S(2)}) copy-start(bf16[16,208,128]{2,1,0:T(8,128)(2,1)S(1)} %collective-permute-done.other_ref) | copy-start | bytes 2555908
  35.4 2.3 %copy-start.1 = (bf16[1,2048,896]{2,1,0:T(8,128)(2,1)S(1)}, bf16[1,2048,896]{2,1,0:T(8,128)(2,1)}, u32[]{:S(2)}) copy-start(bf16[1,2048,896]{2,1,0:T(8,128)(2,1)} %param.17) | copy-start | bytes 11010052
  37.7 2.0 %copy-start.2 = (bf16[1,2048,896]{2,1,0:T(8,128)(2,1)S(1)}, bf16[1,2048,896]{2,1,0:T(8,128)(2,1)}, u32[]{:S(2)}) copy-start(bf16[1,2048,896]{2,1,0:T(8,128)(2,1)} %param.18) | copy-start | bytes 11010052
  39.8 2.0 %copy-start.3 = (bf16[1,896,2048]{2,1,0:T(8,128)(2,1)S(1)}, bf16[1,896,2048]{2,1,0:T(8,128)(2,1)}, u32[]{:S(2)}) copy-start(bf16[1,896,2048]{2,1,0:T(8,128)(2,1)} %param.19) | copy-start | bytes 11010052
  41.8 11.4 %copy-start.7 = (bf16[1,128,128]{2,1,0:T(8,128)(2,1)S(1)}, bf16[1,128,128]{2,1,0:T(8,128)(2,1)}, u32[]{:S(2)}) copy-start(bf16[1,128,128]{2,1,0:T(8,128)(2,1)} %param.11) | copy-start | bytes 98308
  41.8 11.9 %copy-start.8 = (bf16[1,128,128]{2,1,0:T(8,128)(2,1)S(1)}, bf16[1,128,128]{2,1,0:T(8,128)(2,1)}, u32[]{:S(2)}) copy-start(bf16[1,128,128]{2,1,0:T(8,128)(2,1)} %param.12) | copy-start | bytes 98308
  47.0 1.8 %collective-permute-start.1 = (bf16[16,96,128]{2,1,0:T(8,128)(2,1)S(1)}, bf16[16,96,128]{2,1,0:T(8,128)(2,1)S(1)}, u32[]{:S(2)}, u32[]{:S(2)}) collective-permute-start(bf16[16,96,128]{2,1,0:T(8,128)(2,1)S(1)} %get-tuple-element.11), channel_id=1, source_target_pairs={{0,1},{1,0},{2,3},{3,2},{4,5},{5,4},{6,7},{7,6},{8,9},{9,8},{10,11... | collective-permute-start | bytes 1179656 | tf_op jit(solution)/shard_map/ppermute | solution.py:297
  49.6 13.1 %all-to-all-start.1 = ((bf16[16,96,128]{2,1,0:T(8,128)(2,1)}), bf16[16,96,128]{2,1,0:T(8,128)(2,1)S(1)}, u32[]{:S(2)}, u32[]{:S(2)}) async-start(bf16[16,96,128]{2,1,0:T(8,128)(2,1)} %add_convert_fusion), calls=%async_computation.1 | async-start | bytes 786432 | tf_op jit(solution)/shard_map/all_to_all | solution.py:299
  53.2 1.3 %collective-permute-start.2 = (bf16[128,128]{1,0:T(8,128)(2,1)S(1)}, bf16[128,128]{1,0:T(8,128)(2,1)S(1)}, u32[]{:S(2)}, u32[]{:S(2)}) collective-permute-start(bf16[128,128]{1,0:T(8,128)(2,1)S(1)} %bitcast.26), channel_id=1, source_target_pairs={{0,1},{1,0},{2,3},{3,2},{4,5},{5,4},{6,7},{7,6},{8,9},{9,8},{10,11... | collective-permute-start | bytes 98312 | tf_op jit(solution)/shard_map/ppermute | solution.py:268
  53.7 1.2 %collective-permute-start.3 = (bf16[128,128]{1,0:T(8,128)(2,1)S(1)}, bf16[128,128]{1,0:T(8,128)(2,1)S(1)}, u32[]{:S(2)}, u32[]{:S(2)}) collective-permute-start(bf16[128,128]{1,0:T(8,128)(2,1)S(1)} %bitcast.29), channel_id=1, source_target_pairs={{0,1},{1,0},{2,3},{3,2},{4,5},{5,4},{6,7},{7,6},{8,9},{9,8},{10,11... | collective-permute-start | bytes 98312 | tf_op jit(solution)/shard_map/ppermute | solution.py:269
  54.5 0.6 copy-start.9
  55.2 0.6 copy-start.10
  62.7 0.7 copy-start.6
  66.8 7.1 %collective-permute-start.4 = (bf16[128,128]{1,0:T(8,128)(2,1)}, bf16[128,128]{1,0:T(8,128)(2,1)S(1)}, u32[]{:S(2)}, u32[]{:S(2)}) collective-permute-start(bf16[128,128]{1,0:T(8,128)(2,1)} %shard_map.133), channel_id=1, source_target_pairs={{0,224},{32,0},{64,32},{96,64},{128,96},{160,128},{192,160},{224,1... | collective-permute-start | bytes 98312 | tf_op jit(solution)/shard_map/ppermute | solution.py:326

commit v2 on v1

v2 whole, which is shorter than its diff:
```python
import jax
import jax.numpy as jnp
from jax import lax
from jax.experimental import pallas as pl
from jax.experimental.pallas import tpu as pltpu
from jax.sharding import Mesh
from jax.sharding import PartitionSpec as P

MODEL_WIDTH = 2048
EXPERTS = 4
RANK = 16
JOBS = 4
CAP = 80
TOK = 128
COLS = 128
GROUPS = 16
STATS = 48
SEND = 2 * CAP + STATS
BACK = CAP + 16
HIDDEN = 896
EXPERT = ("expert_0", "expert_1")
EXCHANGE = ("expert_1", "expert_0")
EXPERT_DP = ("expert_0", "expert_1", "dp")
EPS = 1e-05
ADAPTER_SCALE = 0.5
F32 = jnp.float32
BF16 = jnp.bfloat16


def dot(a, b, ca, cb):
    return lax.dot_general(a, b, (((ca,), (cb,)), ((), ())), preferred_element_type=F32)


def stand(c):
    return c % 4 * 4 + c // 4


def high_low(v):
    high = v.astype(BF16)
    return high, (v - high.astype(F32)).astype(BF16)


def members(routes):
    label = lax.broadcasted_iota(jnp.int32, (8, TOK), 0)
    member = (label == routes[0:1]) | (label == routes[1:2])
    earlier = (
        lax.broadcasted_iota(jnp.int32, (TOK, TOK), 0)
        < lax.broadcasted_iota(jnp.int32, (TOK, TOK), 1)
    ).astype(BF16)
    rank = dot(member.astype(BF16), earlier, 1, 0)
    return label, member, rank


def owner_mask(lengths, offset, count):
    token = offset + lax.broadcasted_iota(jnp.int32, (JOBS * RANK, count), 1)
    job = lax.broadcasted_iota(jnp.int32, (JOBS * RANK, count), 0) // RANK
    owner = jnp.zeros((JOBS * RANK, count), jnp.int32)
    end = jnp.int32(0)
    for j in range(JOBS):
        end = end + lengths[0, j]
        owner = owner + (token >= end).astype(jnp.int32)
    return owner == job


def local_columns(ref, column):
    return ref[:, pl.ds(pl.multiple_of(column * COLS, COLS), COLS)]


def prepare_kernel(column, block, *refs):
    sources, out_ref, sem = refs[:8], refs[8], refs[17]
    lengths, x_ref, g_ref, routes_ref, gain_ref, router_ref, down_ref, up_ref = refs[9:17]
    copies = [pltpu.make_async_copy(a, b, sem.at[i]) for i, (a, b) in enumerate(zip(sources, refs[9:17]))]
    for copy in copies:
        copy.start()
    for copy in copies:
        copy.wait()
    x = x_ref[...]
    g = g_ref[...]
    _, member, rank = members(routes_ref[...])
    slot = lax.broadcasted_iota(jnp.int32, (CAP, TOK), 0)
    place = jnp.where(member, rank.astype(jnp.int32), -1)
    for e in range(EXPERTS):
        pick = (place[e : e + 1] == slot).astype(BF16)
        xs = dot(pick, x, 1, 0).astype(BF16)
        gs = dot(pick, g, 1, 0).astype(BF16)
        for k in range(GROUPS // EXPERTS):
            out_ref[stand(e * 4 + k), 0:CAP, :] = xs
            out_ref[stand(e * 4 + k), CAP : 2 * CAP, :] = gs
    xf = x.astype(F32)
    xg = (xf * local_columns(gain_ref, column[0])).astype(BF16)
    mask = owner_mask(lengths, block[0] * TOK, TOK)
    low = jnp.where(mask, dot(down_ref[...], xg, 1, 1), 0.0)
    dlow = jnp.where(mask, dot(up_ref[...], g, 1, 1), 0.0)
    low16 = low[0:16] + low[16:32] + low[32:48] + low[48:64]
    dlow16 = dlow[0:16] + dlow[16:32] + dlow[32:48] + dlow[48:64]
    router = local_columns(router_ref, column[0]).astype(F32)
    wide = jnp.concatenate([router, jnp.zeros((4, COLS), F32)], axis=0)
    logits = dot(wide.astype(BF16), xg, 1, 1)
    square = xf * xf
    squares = jnp.sum(square.T, axis=0, keepdims=True)
    row = lax.broadcasted_iota(jnp.int32, (8, TOK), 0)
    small = jnp.where(row == 4, squares, logits)
    high = small.astype(BF16).astype(F32)
    stats = jnp.concatenate([low16, dlow16, high, small - high], axis=0).astype(BF16)
    for k in range(GROUPS):
        out_ref[k, 2 * CAP :, :] = stats


def weights_kernel(gain_ref, *refs):
    sources, gain_out, targets, sem, gain_sem = refs[:3], refs[3], refs[4:7], refs[7], refs[8]
    copies = [pltpu.make_async_copy(gain_ref, gain_out, gain_sem)]
    for i, (source, target) in enumerate(zip(sources, targets)):
        size = source.shape[0] // 4
        for k in range(4):
            rows = slice(k * size, (k + 1) * size)
            copies.append(pltpu.make_async_copy(source.at[rows], target.at[rows], sem.at[i, k]))
    for copy in copies:
        copy.start()
    for copy in copies:
        copy.wait()


CHUNKS = tuple((at, min(256, HIDDEN - at)) for at in range(0, HIDDEN, 256))


def expert_kernel(own_ref, other_ref, gain_ref, wg_ref, wu_ref, wd_ref, own_out, other_out, x_s, g_s, da_s, db_s):
    for d, ref in enumerate((own_ref, other_ref)):
        rows = slice(d * CAP, (d + 1) * CAP)
        total = jnp.zeros((CAP, 128), F32)
        for c in range(GROUPS):
            v = ref[c, 0:CAP, :].astype(F32)
            total = total + v * v
        scale = lax.rsqrt(jnp.sum(total, axis=1, keepdims=True) / MODEL_WIDTH + EPS)
        for c in range(GROUPS):
            cols = slice(c * 128, (c + 1) * 128)
            x_s[rows, cols] = (ref[stand(c), 0:CAP, :].astype(F32) * scale * gain_ref[:, cols]).astype(BF16)
            g_s[rows, cols] = ref[stand(c), CAP : 2 * CAP, :]
    gate_terms = jnp.zeros((2 * CAP, 128), F32)
    stat_terms = jnp.zeros((2 * CAP, 128), F32)
    for lower, size in CHUNKS:
        cols = slice(lower, lower + size)
        a = dot(x_s[...], wg_ref[:, cols], 1, 0)
        b = dot(x_s[...], wu_ref[:, cols], 1, 0)
        back = dot(g_s[...], wd_ref[cols, :], 1, 1)
        sig = jax.nn.sigmoid(a)
        act = a * sig
        da = back * b * sig * (1.0 + a * (1.0 - sig))
        db = back * act
        gate = act * b * back
        stat = da * a + db * b
        for k in range(0, size, 128):
            gate_terms = gate_terms + gate[:, k : k + 128]
            stat_terms = stat_terms + stat[:, k : k + 128]
        da_s[:, cols] = da.astype(BF16)
        db_s[:, cols] = db.astype(BF16)
    lane = lax.broadcasted_iota(jnp.int32, (2 * CAP, 128), 1)
    dgate = jnp.sum(gate_terms, axis=1, keepdims=True)
    dstat = jnp.sum(stat_terms, axis=1, keepdims=True)
    table = jnp.where(lane == 0, dgate, jnp.where(lane == 1, dstat, 0.0))
    row = lax.broadcasted_iota(jnp.int32, (8, 128), 0)
    for d, out in enumerate((own_out, other_out)):
        part = jnp.concatenate([table[d * CAP : (d + 1) * CAP], jnp.zeros((128 - CAP, 128), F32)], axis=0)
        lines = part.T[0:8]
        high = lines.astype(BF16).astype(F32)
        packed = jnp.where(row < 2, high, 0.0) + jnp.where((row >= 2) & (row < 4), jnp.roll(lines - high, 2, 0), 0.0)
        packed = jnp.concatenate([packed, jnp.zeros((8, 128), F32)] if d == 0 else [jnp.zeros((8, 128), F32), packed], axis=0)
        for c in range(GROUPS):
            out[c, CAP:BACK, :] = packed.astype(out.dtype)
    for lower in range(0, MODEL_WIDTH, 256):
        rows = slice(lower, lower + 256)
        dn = dot(da_s[...], wg_ref[rows, :], 1, 1) + dot(db_s[...], wu_ref[rows, :], 1, 1)
        for k in range(2):
            c = lower // 128 + k
            own_out[stand(c), 0:CAP, :] = dn[0:CAP, k * 128 : (k + 1) * 128]
            other_out[stand(c), 0:CAP, :] = dn[CAP:, k * 128 : (k + 1) * 128].astype(BF16)


def stats_kernel(
    column, block, lengths, own_ref, other_ref, x_ref, g_ref, xo_ref, go_ref, routes_ref, gain_ref, down_ref, router_ref,
    grad_down_ref, grad_up_ref, side_ref, base_ref, sb_ref, take_ref, hits_ref, routed_ref,
):
    grad_down = jnp.zeros((JOBS * RANK, COLS), F32)
    grad_up = jnp.zeros((JOBS * RANK, COLS), F32)
    gain = local_columns(gain_ref, column[0])
    row = lax.broadcasted_iota(jnp.int32, (8, TOK), 0)
    for d, (ref, xr, gr) in enumerate(((own_ref, x_ref, g_ref), (other_ref, xo_ref, go_ref))):
        total = ref[0, 2 * CAP :, :].astype(F32)
        for c in range(1, GROUPS):
            total = total + ref[c, 2 * CAP :, :].astype(F32)
        small = total[32:40] + total[40:48]
        scale = lax.rsqrt(small[4:5] / MODEL_WIDTH + EPS)
        mask = owner_mask(lengths, (block[0] if d == 0 else 1 - block[0]) * TOK, TOK)
        low16 = total[0:16]
        dlow16 = ADAPTER_SCALE * total[16:32]
        low = jnp.where(mask, jnp.concatenate([low16 * scale] * JOBS, axis=0), 0.0).astype(BF16)
        dlow = jnp.where(mask, jnp.concatenate([dlow16] * JOBS, axis=0), 0.0).astype(BF16)
        if d == 0:
            routes = routes_ref[...]
            label, member, rank = members(routes)
            first = label == routes[0:1]
            second = label == routes[1:2]
            raw = jnp.sum(jnp.where(first, small, 0.0) - jnp.where(second, small, 0.0), axis=0, keepdims=True)
            upper = jax.nn.sigmoid(raw * scale)
            adapter_stat = jnp.sum(dlow16.astype(BF16).astype(F32) * low16, axis=0, keepdims=True)
            at1 = jnp.sum(jnp.where(first, rank, 0.0), axis=0, keepdims=True)
            at2 = jnp.sum(jnp.where(second, rank, 0.0), axis=0, keepdims=True)
            lines = [scale, adapter_stat, raw, upper, at1, at2, routes[0:1].astype(F32), routes[1:2].astype(F32)]
        else:
            lines = [scale] * 8
        packed = jnp.zeros((8, TOK), F32)
        for k, line in enumerate(lines):
            packed = jnp.where(row == k, line, packed)
        side = jnp.concatenate([packed, jnp.zeros((120, TOK), F32)], axis=0).T
        scale_col = side[:, 0:1]
        xf = xr[...].astype(F32)
        normed = (xf * scale_col * gain).astype(BF16)
        grad_down = grad_down + dot(dlow, normed, 1, 0)
        grad_up = grad_up + dot(low, gr[...], 1, 0)
        if d == 0:
            side_ref[...] = side
            wide = jnp.concatenate([down_ref[...].astype(F32), jnp.zeros((64, COLS), F32)], axis=0)
            adapter = dot(wide.T.astype(BF16)[:, 0 : JOBS * RANK], dlow, 1, 0).T
            base_ref[...] = gr[...].astype(F32) + scale_col * adapter * gain
            sb_ref[...] = xf * scale_col * scale_col * scale_col / MODEL_WIDTH
            lane = lax.broadcasted_iota(jnp.int32, (TOK, 128), 1)
            upper = side[:, 3:4]
            at1, at2 = side[:, 4:5].astype(jnp.int32), side[:, 5:6].astype(jnp.int32)
            first, second = side[:, 6:7].astype(jnp.int32), side[:, 7:8].astype(jnp.int32)
            router = local_columns(router_ref, column[0]).astype(F32)
            routed = jnp.zeros((TOK, COLS), F32)
            for e in range(EXPERTS):
                hit1 = ((lane == at1) & (first == e)).astype(F32)
                hit2 = ((lane == at2) & (second == e)).astype(F32)
                take = upper * hit1 + (1.0 - upper) * hit2
                high = take.astype(BF16)
                take_ref[0, e] = high
                take_ref[1, e] = (take - high.astype(F32)).astype(BF16)
                hits_ref[0, e] = take
                hits_ref[1, e] = hit1 - hit2
                sign = (first == e).astype(F32) - (second == e).astype(F32)
                routed = routed + sign * router[e : e + 1]
            routed_ref[...] = routed
    grad_down_ref[...] = grad_down
    grad_up_ref[...] = ADAPTER_SCALE * grad_up


def finish_kernel(column, in_ref, gain_ref, side_ref, base_ref, sb_ref, take_ref, hits_ref, routed_ref, out_ref):
    side = side_ref[...]
    scale, adapter_stat, raw, upper = (side[:, k : k + 1] for k in range(4))
    rows = jnp.zeros((TOK, COLS), F32)
    spread = jnp.zeros((TOK, 128), F32)
    stat = jnp.zeros((TOK, 128), F32)
    for e in range(EXPERTS):
        total = in_ref[stand(4 * e)].astype(F32)
        for k in range(1, 4):
            total = total + in_ref[stand(4 * e + k)].astype(F32)
        lines = total[CAP : CAP + 8] + total[CAP + 8 : CAP + 16]
        spread = spread + hits_ref[1, e] * (lines[0:1] + lines[2:3])
        stat = stat + hits_ref[0, e] * (lines[1:2] + lines[3:4])
        high, low = high_low(total[0:CAP])
        take = take_ref[0, e, :, 0:CAP]
        rows = rows + dot(take, high, 1, 0) + dot(take, low, 1, 0) + dot(take_ref[1, e, :, 0:CAP], high, 1, 0)
    delta = jnp.sum(spread, axis=1, keepdims=True) * upper * (1.0 - upper)
    stat = jnp.sum(stat, axis=1, keepdims=True) / scale + adapter_stat + delta * raw
    dnormed = rows + delta * routed_ref[...]
    result = base_ref[...] + scale * dnormed * local_columns(gain_ref, column[0]) - sb_ref[...] * stat
    out_ref[...] = result.astype(BF16)


VMEM = pl.BlockSpec(memory_space=pltpu.VMEM)
SMEM = pl.BlockSpec(memory_space=pltpu.SMEM)
HBM = pl.BlockSpec(memory_space=pltpu.HBM)


def pinned(v):
    return pltpu.with_memory_space_constraint(v, pltpu.HBM)


def call(kernel, out_shape, scalars, args, scratch=(), arg_specs=None):
    return pl.pallas_call(
        kernel,
        in_specs=[SMEM] * len(scalars) + (arg_specs or [VMEM] * len(args)),
        out_specs=VMEM if isinstance(out_shape, jax.ShapeDtypeStruct) else (VMEM,) * len(out_shape),
        out_shape=out_shape,
        scratch_shapes=scratch,
        compiler_params=pltpu.CompilerParams(vmem_limit_bytes=32 * 1024 * 1024),
    )(*scalars, *(pinned(v) if spec is HBM else v for v, spec in zip(args, arg_specs or [VMEM] * len(args))))


def shards(stash, cotangent, routes, lengths, gains, router, wg, wu, wd, down, up):
    x, g = stash[0], cotangent[0]
    routes, router, down = routes[0].T, router[0].T, down[0].T
    wg, wu, wd, up = wg[0], wu[0], wd[0], up[0]
    shape = jax.ShapeDtypeStruct
    column = lax.axis_index(EXPERT).astype(jnp.int32).reshape(1)
    block = lax.axis_index("dp").astype(jnp.int32).reshape(1)
    swap = [(0, 1), (1, 0)]
    xo = lax.ppermute(x, "dp", swap)
    go = lax.ppermute(g, "dp", swap)
    locals_ = (lengths, x, g, routes, gains, router, down, up)
    sent = call(
        prepare_kernel,
        shape((GROUPS, SEND, 128), BF16),
        (column, block),
        locals_,
        [pltpu.SMEM(lengths.shape, jnp.int32)]
        + [pltpu.VMEM(v.shape, v.dtype) for v in locals_[1:]]
        + [pltpu.SemaphoreType.DMA((8,))],
        [HBM] * 8,
    )
    own = lax.all_to_all(sent, EXCHANGE, 0, 0, tiled=True)
    other = lax.ppermute(own, "dp", swap)
    gains_here, *weights = call(
        weights_kernel,
        tuple(shape(v.shape, v.dtype) for v in (gains, wg, wu, wd)),
        (),
        (gains, wg, wu, wd),
        [pltpu.SemaphoreType.DMA((3, 4)), pltpu.SemaphoreType.DMA],
        [HBM] * 4,
    )
    own_part, other_part = call(
        expert_kernel,
        (shape((GROUPS, BACK, 128), F32), shape((GROUPS, BACK, 128), BF16)),
        (),
        (own, other, gains_here, *weights),
        [
            pltpu.VMEM((2 * CAP, MODEL_WIDTH), BF16),
            pltpu.VMEM((2 * CAP, MODEL_WIDTH), BF16),
            pltpu.VMEM((2 * CAP, HIDDEN), BF16),
            pltpu.VMEM((2 * CAP, HIDDEN), BF16),
        ],
    )
    arrived = lax.ppermute(other_part, "dp", swap)
    parts = (own_part + arrived.astype(F32)).astype(BF16)
    back = lax.all_to_all(parts, EXCHANGE, 0, 0, tiled=True)
    small = shape((JOBS * RANK, COLS), F32)
    square = shape((TOK, COLS), F32)
    grad_down, grad_up, side, base, sb, take, hits, routed = call(
        stats_kernel,
        (
            small, small, square, square, square,
            shape((2, EXPERTS, TOK, 128), BF16), shape((2, EXPERTS, TOK, 128), F32), square,
        ),
        (column, block, lengths),
        (own, other, x, g, xo, go, routes, gains, down, router),
    )
    result = call(
        finish_kernel,
        shape((TOK, COLS), BF16),
        (column,),
        (back, gains, side, base, sb, take, hits, routed),
    )
    count = lax.axis_size("section")
    handed = lax.ppermute(result, "section", [(i, (i - 1) % count) for i in range(count)])
    return handed[None], grad_down.T[None], grad_up[None]


def solution(mesh):
    finer = Mesh(
        mesh.devices.reshape(mesh.shape["section"], 4, 4, mesh.shape["dp"]),
        ("section", "expert_0", "expert_1", "dp"),
    )
    in_specs = (
        P("section", "dp", EXPERT),
        P("section", "dp", EXPERT),
        P("section", "dp", None),
        P("section", None),
        P("section", None),
        P("section", None, None),
        P("section", None, EXPERT_DP),
        P("section", None, EXPERT_DP),
        P("section", EXPERT_DP, None),
        P("section", EXPERT, None),
        P("section", None, EXPERT),
    )
    out_specs = (P("section", "dp", EXPERT), P("section", EXPERT, None), P("section", None, EXPERT))
    return jax.shard_map(shards, mesh=finer, in_specs=in_specs, out_specs=out_specs, check_vma=False)
```

time: 75.2 us -> 58.3 us (0.78)
  local copies, waits for them, and re-layouts: 14.8 us -> 0.66 us
  Pallas kernels: 15 us -> 13.5 us
  other arithmetic: 2.11 us -> 0.85 us
  waiting for transfers between devices: 8.14 us -> 9.26 us
    unnamed x27 -> x15, local copies, waits for them, and re-layouts: 14.8 us -> 0.66 us
    ppermute x1, waiting for transfers between devices: 2.01 us -> 0.01 us  [shards(): other = lax.ppermute(own, 'dp', swap)]
    all_to_all x1, waiting for transfers between devices: 3.71 us -> 5.51 us  [shards(): back = lax.all_to_all(parts, EXCHANGE, 0, 0, tiled=True)]
    pallas_call x4 -> x5, Pallas kernels: 15 us -> 13.5 us  [call(): pl.pallas_call(kernel, in_specs=[SMEM] * len(scalars) + (arg_specs or [VM...]
    concatenate x1 -> x0, other arithmetic: 1.29 us -> none  [shards(): jnp.concatenate([jnp.stack([lax.axis_index(EXPERT), lax.axis_index('dp')]...]
    ppermute x1, waiting for transfers between devices: 0.01 us -> 1.02 us  [shards(): lax.ppermute(result, 'section', [(i, (i - 1) % count) for i in range(coun...]
  transfers between devices with their start and end apart: 6 -> 6, of which waited for: 5 -> 5; matrix products, arithmetic and copies ran while one was open for 2% -> 0% of each run, Pallas kernels for 4% -> 11%
where the time goes in v2:
time: 58.3 us; the launch traced here: 58 us
  blocking collectives  21.3 us (37%)
  Pallas kernels  13.5 us (23%)
  starting transfers between devices  11.8 us (20%)
  waiting for transfers between devices  9.26 us (16%)
  other arithmetic  0.85 us (1%)
  between operations  0.78 us (1%)
  local copies, waits for them, and re-layouts  0.66 us (1%)
    all_to_all x1, blocking collectives, shards(): own = lax.all_to_all(sent, EXCHANGE, 0, 0, tiled=True)  21.3 us
    pallas_call x5, Pallas kernels, call(): pl.pallas_call(kernel, in_specs=[SMEM] * len(scalars) + (arg_specs or [VM...  13.5 us
    ppermute x1, starting transfers between devices, shards(): lax.ppermute(result, 'section', [(i, (i - 1) % count) for i in range(coun...  5.65 us
    all_to_all x1, waiting for transfers between devices, shards(): back = lax.all_to_all(parts, EXCHANGE, 0, 0, tiled=True)  5.51 us
    all_to_all x1, starting transfers between devices, shards(): back = lax.all_to_all(parts, EXCHANGE, 0, 0, tiled=True)  3.55 us
    ppermute x1, starting transfers between devices, shards(): other = lax.ppermute(own, 'dp', swap)  1.86 us
    ppermute x1, waiting for transfers between devices, shards(): arrived = lax.ppermute(other_part, 'dp', swap)  1.71 us
  transfers between devices with their start and end apart: 6, of which 5 were waited for; matrix products, arithmetic and copies ran while one was open for 0% of the time, Pallas kernels for 11%

profile of v2, /device:TPU:1, one launch (start us, length us, event | category | flops | bytes accessed | tf_op | source)
XLA Modules:
  0.0 58.0 jit_solution(1721587551580221565)
XLA Ops:
  0.6 1.3 %shard_map.130 = bf16[16,208,128]{2,1,0:T(8,128)(2,1)S(1)} custom-call(s32[1]{0:T(128)} %bitcast.column, s32[1]{0:T(128)} %bitcast.1.block, s32[1,4]{1,0:T(1,128)} %lengths.1, bf16[128,128]{1,0:T(8,128)(2,1)} %bitcast.22, bf16[128,128]{1,0:T(8,128)(2,1)} %bitcast.25, s32[2,128]{1,0:T(2,128)} %bitcast.32, f32[1,2048]{1,0:T(1,128)} %gain_ref.5, ...), custom_call_target="tpu_custom_call" | custom-call | tf_op jit(solution)/shard_map/pallas_call | solution.py:280
  2.0 21.3 %all_to_all.10.own_ref = bf16[16,208,128]{2,1,0:T(8,128)(2,1)S(1)} all-to-all(bf16[16,208,128]{2,1,0:T(8,128)(2,1)S(1)} %shard_map.130), channel_id=1, replica_groups=mesh['section'=8,'expert_0'=4,'expert_1'=4,'dp'=2] {'expert_1','expert_0'}, dimensions={0} | all-to-all | bytes 1703936 | tf_op jit(solution)/shard_map/all_to_all | solution.py:311
  23.2 1.9 %collective-permute-start = (bf16[16,208,128]{2,1,0:T(8,128)(2,1)S(1)}, bf16[16,208,128]{2,1,0:T(8,128)(2,1)S(1)}, u32[]{:S(2)}, u32[]{:S(2)}) collective-permute-start(bf16[16,208,128]{2,1,0:T(8,128)(2,1)S(1)} %all_to_all.10.own_ref), channel_id=1, source_target_pairs={{0,1},{1,0},{2,3},{3,2},{4,5},{5,4},{6,7},{7,6},{8,9},{9,8},{10,11... | collective-permute-start | bytes 2555912 | tf_op jit(solution)/shard_map/ppermute | solution.py:312
  25.1 4.3 %shard_map.131 = (f32[1,2048]{1,0:T(1,128)S(1)}, bf16[2048,896]{1,0:T(8,128)(2,1)S(1)}, bf16[2048,896]{1,0:T(8,128)(2,1)S(1)}, bf16[896,2048]{1,0:T(8,128)(2,1)S(1)}) custom-call(f32[1,2048]{1,0:T(1,128)} %gain_ref.5, bf16[2048,896]{1,0:T(8,128)(2,1)} %bitcast.34, bf16[2048,896]{1,0:T(8,128)(2,1)} %bitcast.35, bf16[896,2048]{1,0:T(8,128)(2,1)} %bitcast.36), custom_call_target="tpu_custom_call" | custom-call | tf_op jit(solution)/shard_map/pallas_call | solution.py:280
  29.4 0.0 copy-start.1
  29.4 0.0 copy-start.2
  29.4 0.0 copy-start.3
  29.4 0.0 copy-start.4
  29.4 0.0 copy-start.6
  29.4 5.4 %shard_map.132 = (f32[16,96,128]{2,1,0:T(8,128)S(1)}, bf16[16,96,128]{2,1,0:T(8,128)(2,1)S(1)}) custom-call(bf16[16,208,128]{2,1,0:T(8,128)(2,1)S(1)} %all_to_all.10.own_ref, bf16[16,208,128]{2,1,0:T(8,128)(2,1)S(1)} %collective-permute-done.other_ref, f32[1,2048]{1,0:T(1,128)S(1)} %get-tuple-element.17.gain_ref, ...), custom_call_target="tpu_custom_call" | custom-call | tf_op jit(solution)/shard_map/pallas_call | solution.py:280
  34.9 0.1 collective-permute-start.1
  35.0 1.7 %collective-permute-done.1 = bf16[16,96,128]{2,1,0:T(8,128)(2,1)S(1)} collective-permute-done((bf16[16,96,128]{2,1,0:T(8,128)(2,1)S(1)}, bf16[16,96,128]{2,1,0:T(8,128)(2,1)S(1)}, u32[]{:S(2)}, u32[]{:S(2)}) %collective-permute-start.1) | collective-permute-done | bytes 393248 | tf_op jit(solution)/shard_map/ppermute | solution.py:333
  36.7 0.9 %add_convert_fusion = bf16[16,96,128]{2,1,0:T(8,128)(2,1)} fusion(f32[16,96,128]{2,1,0:T(8,128)S(1)} %get-tuple-element.21, bf16[16,96,128]{2,1,0:T(8,128)(2,1)S(1)} %collective-permute-done.1), kind=kLoop, calls=%fused_computation | loop fusion | flops 589824 | bytes 1572864 | tf_op jit(solution)/shard_map/convert_element_type | solution.py:334
  37.5 3.6 %all-to-all-start.1 = ((bf16[16,96,128]{2,1,0:T(8,128)(2,1)}), bf16[16,96,128]{2,1,0:T(8,128)(2,1)S(1)}, u32[]{:S(2)}, u32[]{:S(2)}) async-start(bf16[16,96,128]{2,1,0:T(8,128)(2,1)} %add_convert_fusion), calls=%async_computation.1 | async-start | bytes 786432 | tf_op jit(solution)/shard_map/all_to_all | solution.py:335
  41.1 0.4 collective-permute-start.2
  41.5 0.2 collective-permute-start.3
  41.7 0.7 %collective-permute-done.2.xo_ref = bf16[128,128]{1,0:T(8,128)(2,1)S(1)} collective-permute-done((bf16[128,128]{1,0:T(8,128)(2,1)S(1)}, bf16[128,128]{1,0:T(8,128)(2,1)S(1)}, u32[]{:S(2)}, u32[]{:S(2)}) %collective-permute-start.2) | collective-permute-done | bytes 32800 | tf_op jit(solution)/shard_map/ppermute | solution.py:298
  42.4 0.3 collective-permute-done.3.go_ref
  42.8 2.1 %shard_map.133 = (f32[64,128]{1,0:T(8,128)}, f32[64,128]{1,0:T(8,128)}, f32[128,128]{1,0:T(8,128)S(1)}, f32[128,128]{1,0:T(8,128)S(1)}, f32[128,128]{1,0:T(8,128...) custom-call(s32[1]{0:T(128)} %bitcast.column, ...), custom_call_target="tpu_custom_call" | custom-call | tf_op jit(solution)/shard_map/pallas_call | solution.py:280
  44.9 5.5 %all-to-all-done.1.in_ref = bf16[16,96,128]{2,1,0:T(8,128)(2,1)S(1)} async-done(((bf16[16,96,128]{2,1,0:T(8,128)(2,1)}), bf16[16,96,128]{2,1,0:T(8,128)(2,1)S(1)}, u32[]{:S(2)}, u32[]{:S(2)}) %all-to-all-start.1) | async-done | bytes 393248 | tf_op jit(solution)/shard_map/all_to_all | solution.py:335
  50.4 0.3 shard_map.134
  50.8 5.6 %collective-permute-start.4 = (bf16[128,128]{1,0:T(8,128)(2,1)S(1)}, bf16[128,128]{1,0:T(8,128)(2,1)S(1)}, u32[]{:S(2)}, u32[]{:S(2)}) collective-permute-start(bf16[128,128]{1,0:T(8,128)(2,1)S(1)} %shard_map.134), channel_id=1, source_target_pairs={{0,224},{32,0},{64,32},{96,64},{128,96},{160,128},{192,160},{224,1... | collective-permute-start | bytes 98312 | tf_op jit(solution)/shard_map/ppermute | solution.py:354
  56.4 1.0 %collective-permute-done.4 = bf16[128,128]{1,0:T(8,128)(2,1)S(1)} collective-permute-done((bf16[128,128]{1,0:T(8,128)(2,1)S(1)}, bf16[128,128]{1,0:T(8,128)(2,1)S(1)}, u32[]{:S(2)}, u32[]{:S(2)}) %collective-permute-start.4) | collective-permute-done | bytes 32800 | tf_op jit(solution)/shard_map/ppermute | solution.py:354
  57.4 0.6 %copy.15 = bf16[1,128,128]{2,1,0:T(8,128)(2,1)} copy(bf16[1,128,128]{2,1,0:T(8,128)(2,1)S(1)} %bitcast.37) | data formatting | bytes 65536
  (10 shorter events, 0.0 us)
Async XLA Ops:
  23.2 6.1 %collective-permute-start = (bf16[16,208,128]{2,1,0:T(8,128)(2,1)S(1)}, bf16[16,208,128]{2,1,0:T(8,128)(2,1)S(1)}, u32[]{:S(2)}, u32[]{:S(2)}) collective-permute-start(bf16[16,208,128]{2,1,0:T(8,128)(2,1)S(1)} %all_to_all.10.own_ref), channel_id=1, source_target_pairs={{0,1},{1,0},{2,3},{3,2},{4,5},{5,4},{6,7},{7,6},{8,9},{9,8},{10,11... | collective-permute-start | bytes 2555912 | tf_op jit(solution)/shard_map/ppermute | solution.py:312
  29.4 11.7 %copy-start.1 = (bf16[1,128,128]{2,1,0:T(8,128)(2,1)S(1)}, bf16[1,128,128]{2,1,0:T(8,128)(2,1)}, u32[]{:S(2)}) copy-start(bf16[1,128,128]{2,1,0:T(8,128)(2,1)} %param.11) | copy-start | bytes 98308
  29.4 12.1 %copy-start.2 = (bf16[1,128,128]{2,1,0:T(8,128)(2,1)S(1)}, bf16[1,128,128]{2,1,0:T(8,128)(2,1)}, u32[]{:S(2)}) copy-start(bf16[1,128,128]{2,1,0:T(8,128)(2,1)} %param.12) | copy-start | bytes 98308
  29.4 13.3 %copy-start = (f32[1,2048]{1,0:T(1,128)S(1)}, f32[1,2048]{1,0:T(1,128)}, u32[]{:S(2)}) copy-start(f32[1,2048]{1,0:T(1,128)} %gain_ref.5) | copy-start | bytes 24580
  29.4 13.3 %copy-start.3 = (bf16[1,2048,4]{1,2,0:T(4,128)(2,1)S(1)}, bf16[1,2048,4]{1,2,0:T(4,128)(2,1)}, u32[]{:S(2)}) copy-start(bf16[1,2048,4]{1,2,0:T(4,128)(2,1)} %param.16) | copy-start | bytes 49156
  29.4 13.3 %copy-start.4 = (bf16[1,128,64]{1,2,0:T(8,128)(2,1)S(1)}, bf16[1,128,64]{1,2,0:T(8,128)(2,1)}, u32[]{:S(2)}) copy-start(bf16[1,128,64]{1,2,0:T(8,128)(2,1)} %param.20) | copy-start | bytes 49156
  29.4 13.3 %copy-start.5 = (s32[1,128,2]{1,2,0:T(2,128)S(1)}, s32[1,128,2]{1,2,0:T(2,128)}, u32[]{:S(2)}) copy-start(s32[1,128,2]{1,2,0:T(2,128)} %param.13) | copy-start | bytes 3076
  29.4 13.3 %copy-start.6 = (s32[1,4]{1,0:T(1,128)S(1)}, s32[1,4]{1,0:T(1,128)}, u32[]{:S(2)}) copy-start(s32[1,4]{1,0:T(1,128)} %lengths.1) | copy-start | bytes 52
  34.9 1.8 %collective-permute-start.1 = (bf16[16,96,128]{2,1,0:T(8,128)(2,1)S(1)}, bf16[16,96,128]{2,1,0:T(8,128)(2,1)S(1)}, u32[]{:S(2)}, u32[]{:S(2)}) collective-permute-start(bf16[16,96,128]{2,1,0:T(8,128)(2,1)S(1)} %get-tuple-element.22), channel_id=1, source_target_pairs={{0,1},{1,0},{2,3},{3,2},{4,5},{5,4},{6,7},{7,6},{8,9},{9,8},{10,11... | collective-permute-start | bytes 1179656 | tf_op jit(solution)/shard_map/ppermute | solution.py:333
  37.5 12.9 %all-to-all-start.1 = ((bf16[16,96,128]{2,1,0:T(8,128)(2,1)}), bf16[16,96,128]{2,1,0:T(8,128)(2,1)S(1)}, u32[]{:S(2)}, u32[]{:S(2)}) async-start(bf16[16,96,128]{2,1,0:T(8,128)(2,1)} %add_convert_fusion), calls=%async_computation.1 | async-start | bytes 786432 | tf_op jit(solution)/shard_map/all_to_all | solution.py:335
  41.1 1.3 %collective-permute-start.2 = (bf16[128,128]{1,0:T(8,128)(2,1)S(1)}, bf16[128,128]{1,0:T(8,128)(2,1)S(1)}, u32[]{:S(2)}, u32[]{:S(2)}) collective-permute-start(bf16[128,128]{1,0:T(8,128)(2,1)S(1)} %bitcast.23), channel_id=1, source_target_pairs={{0,1},{1,0},{2,3},{3,2},{4,5},{5,4},{6,7},{7,6},{8,9},{9,8},{10,11... | collective-permute-start | bytes 98312 | tf_op jit(solution)/shard_map/ppermute | solution.py:298
  41.5 1.2 %collective-permute-start.3 = (bf16[128,128]{1,0:T(8,128)(2,1)S(1)}, bf16[128,128]{1,0:T(8,128)(2,1)S(1)}, u32[]{:S(2)}, u32[]{:S(2)}) collective-permute-start(bf16[128,128]{1,0:T(8,128)(2,1)S(1)} %bitcast.26), channel_id=1, source_target_pairs={{0,1},{1,0},{2,3},{3,2},{4,5},{5,4},{6,7},{7,6},{8,9},{9,8},{10,11... | collective-permute-start | bytes 98312 | tf_op jit(solution)/shard_map/ppermute | solution.py:299
  50.8 6.7 %collective-permute-start.4 = (bf16[128,128]{1,0:T(8,128)(2,1)S(1)}, bf16[128,128]{1,0:T(8,128)(2,1)S(1)}, u32[]{:S(2)}, u32[]{:S(2)}) collective-permute-start(bf16[128,128]{1,0:T(8,128)(2,1)S(1)} %shard_map.134), channel_id=1, source_target_pairs={{0,224},{32,0},{64,32},{96,64},{128,96},{160,128},{192,160},{224,1... | collective-permute-start | bytes 98312 | tf_op jit(solution)/shard_map/ppermute | solution.py:354

commit v3 on v2

--- a/solution.py
+++ b/solution.py
@@ -18,6 +18,7 @@
 SEND = 2 * CAP + STATS
 BACK = CAP + 16
 HIDDEN = 896
+EARLY = 256
 EXPERT = ("expert_0", "expert_1")
 EXCHANGE = ("expert_1", "expert_0")
 EXPERT_DP = ("expert_0", "expert_1", "dp")
@@ -67,10 +68,16 @@
 
 
 def prepare_kernel(column, block, *refs):
-    sources, out_ref, sem = refs[:8], refs[8], refs[17]
-    lengths, x_ref, g_ref, routes_ref, gain_ref, router_ref, down_ref, up_ref = refs[9:17]
-    copies = [pltpu.make_async_copy(a, b, sem.at[i]) for i, (a, b) in enumerate(zip(sources, refs[9:17]))]
+    sources, wd_hbm, out_ref, early_ref, sem = refs[:8], refs[8], refs[9], refs[10], refs[19]
+    lengths, x_ref, g_ref, routes_ref, gain_ref, router_ref, down_ref, up_ref = refs[11:19]
+    copies = [pltpu.make_async_copy(a, b, sem.at[i]) for i, (a, b) in enumerate(zip(sources, refs[11:19]))]
+    early = []
+    for k in range(EARLY // 128):
+        rows = slice(k * 128, (k + 1) * 128)
+        early.append(pltpu.make_async_copy(wd_hbm.at[rows], early_ref.at[rows], sem.at[8 + k]))
     for copy in copies:
+        copy.start()
+    for copy in early:
         copy.start()
     for copy in copies:
         copy.wait()
@@ -104,16 +111,19 @@
     stats = jnp.concatenate([low16, dlow16, high, small - high], axis=0).astype(BF16)
     for k in range(GROUPS):
         out_ref[k, 2 * CAP :, :] = stats
+    for copy in early:
+        copy.wait()
 
 
 def weights_kernel(gain_ref, *refs):
     sources, gain_out, targets, sem, gain_sem = refs[:3], refs[3], refs[4:7], refs[7], refs[8]
     copies = [pltpu.make_async_copy(gain_ref, gain_out, gain_sem)]
     for i, (source, target) in enumerate(zip(sources, targets)):
-        size = source.shape[0] // 4
+        skipped = source.shape[0] - target.shape[0]
+        size = target.shape[0] // 4
         for k in range(4):
-            rows = slice(k * size, (k + 1) * size)
-            copies.append(pltpu.make_async_copy(source.at[rows], target.at[rows], sem.at[i, k]))
+            there, here = slice(skipped + k * size, skipped + (k + 1) * size), slice(k * size, (k + 1) * size)
+            copies.append(pltpu.make_async_copy(source.at[there], target.at[here], sem.at[i, k]))
     for copy in copies:
         copy.start()
     for copy in copies:
@@ -123,7 +133,7 @@
 CHUNKS = tuple((at, min(256, HIDDEN - at)) for at in range(0, HIDDEN, 256))
 
 
-def expert_kernel(own_ref, other_ref, gain_ref, wg_ref, wu_ref, wd_ref, own_out, other_out, x_s, g_s, da_s, db_s):
+def expert_kernel(own_ref, other_ref, gain_ref, wg_ref, wu_ref, wd_ref, early_ref, own_out, other_out, x_s, g_s, da_s, db_s):
     for d, ref in enumerate((own_ref, other_ref)):
         rows = slice(d * CAP, (d + 1) * CAP)
         total = jnp.zeros((CAP, 128), F32)
@@ -141,7 +151,8 @@
         cols = slice(lower, lower + size)
         a = dot(x_s[...], wg_ref[:, cols], 1, 0)
         b = dot(x_s[...], wu_ref[:, cols], 1, 0)
-        back = dot(g_s[...], wd_ref[cols, :], 1, 1)
+        wd = early_ref[cols, :] if lower < EARLY else wd_ref[lower - EARLY : lower - EARLY + size, :]
+        back = dot(g_s[...], wd, 1, 1)
         sig = jax.nn.sigmoid(a)
         act = a * sig
         da = back * b * sig * (1.0 + a * (1.0 - sig))
@@ -298,31 +309,35 @@
     xo = lax.ppermute(x, "dp", swap)
     go = lax.ppermute(g, "dp", swap)
     locals_ = (lengths, x, g, routes, gains, router, down, up)
-    sent = call(
+    sent, early = call(
         prepare_kernel,
-        shape((GROUPS, SEND, 128), BF16),
+        (shape((GROUPS, SEND, 128), BF16), shape((EARLY, MODEL_WIDTH), BF16)),
         (column, block),
-        locals_,
+        (*locals_, wd),
         [pltpu.SMEM(lengths.shape, jnp.int32)]
         + [pltpu.VMEM(v.shape, v.dtype) for v in locals_[1:]]
-        + [pltpu.SemaphoreType.DMA((8,))],
-        [HBM] * 8,
+        + [pltpu.SemaphoreType.DMA((8 + EARLY // 128,))],
+        [HBM] * 9,
     )
     own = lax.all_to_all(sent, EXCHANGE, 0, 0, tiled=True)
     other = lax.ppermute(own, "dp", swap)
     gains_here, *weights = call(
         weights_kernel,
-        tuple(shape(v.shape, v.dtype) for v in (gains, wg, wu, wd)),
+        (
+            shape(gains.shape, F32), shape(wg.shape, BF16), shape(wu.shape, BF16),
+            shape((HIDDEN - EARLY, MODEL_WIDTH), BF16),
+        ),
         (),
         (gains, wg, wu, wd),
         [pltpu.SemaphoreType.DMA((3, 4)), pltpu.SemaphoreType.DMA],
         [HBM] * 4,
     )
+    other, xo, go = lax.optimization_barrier((other, xo, go))
     own_part, other_part = call(
         expert_kernel,
         (shape((GROUPS, BACK, 128), F32), shape((GROUPS, BACK, 128), BF16)),
         (),
-        (own, other, gains_here, *weights),
+        (own, other, gains_here, *weights, early),
         [
             pltpu.VMEM((2 * CAP, MODEL_WIDTH), BF16),
             pltpu.VMEM((2 * CAP, MODEL_WIDTH), BF16),
@@ -331,8 +346,6 @@
         ],
     )
     arrived = lax.ppermute(other_part, "dp", swap)
-    parts = (own_part + arrived.astype(F32)).astype(BF16)
-    back = lax.all_to_all(parts, EXCHANGE, 0, 0, tiled=True)
     small = shape((JOBS * RANK, COLS), F32)
     square = shape((TOK, COLS), F32)
     grad_down, grad_up, side, base, sb, take, hits, routed = call(
@@ -344,6 +357,9 @@
         (column, block, lengths),
         (own, other, x, g, xo, go, routes, gains, down, router),
     )
+    arrived, side = lax.optimization_barrier((arrived, side))
+    parts = (own_part + arrived.astype(F32)).astype(BF16)
+    back = lax.all_to_all(parts, EXCHANGE, 0, 0, tiled=True)
     result = call(
         finish_kernel,
         shape((TOK, COLS), BF16),

time: 58.3 us -> 57.8 us (level)
  blocking collectives: 21.3 us -> 33.6 us
  waiting for transfers between devices: 9.26 us -> 1.03 us
  starting transfers between devices: 11.8 us -> 8.24 us
  other arithmetic: 0.85 us -> 0.1 us
    all_to_all x0 -> x1, blocking collectives: none -> 12.4 us  [shards(): back = lax.all_to_all(parts, EXCHANGE, 0, 0, tiled=True)]
    all_to_all x1 -> x0, waiting for transfers between devices: 5.51 us -> none  [shards(): back = lax.all_to_all(parts, EXCHANGE, 0, 0, tiled=True)]
    all_to_all x1 -> x0, starting transfers between devices: 3.55 us -> none  [shards(): back = lax.all_to_all(parts, EXCHANGE, 0, 0, tiled=True)]
    ppermute x1, waiting for transfers between devices: 1.71 us -> 0.01 us  [shards(): arrived = lax.ppermute(other_part, 'dp', swap)]
    convert_element_type x1, other arithmetic: 0.85 us -> 0.1 us  [shards(): parts = (own_part + arrived.astype(F32)).astype(BF16)]
    ppermute x1, waiting for transfers between devices: 0.69 us -> 0.01 us  [shards(): xo = lax.ppermute(x, 'dp', swap)]
  transfers between devices with their start and end apart: 6 -> 5, of which waited for: 5 -> 1; matrix products, arithmetic and copies ran while one was open for 0% -> 0% of each run, Pallas kernels for 11% -> 11%
where the time goes in v3:
time: 57.8 us; the launch traced here: 57.6 us
  blocking collectives  33.6 us (58%)
  Pallas kernels  13.2 us (23%)
  starting transfers between devices  8.24 us (14%)
  waiting for transfers between devices  1.03 us (2%)
  between operations  0.77 us (1%)
  local copies, waits for them, and re-layouts  0.65 us (1%)
    all_to_all x1, blocking collectives, shards(): own = lax.all_to_all(sent, EXCHANGE, 0, 0, tiled=True)  21.3 us
    pallas_call x5, Pallas kernels, call(): pl.pallas_call(kernel, in_specs=[SMEM] * len(scalars) + (arg_specs or [VM...  13.2 us
    all_to_all x1, blocking collectives, shards(): back = lax.all_to_all(parts, EXCHANGE, 0, 0, tiled=True)  12.4 us
    ppermute x1, starting transfers between devices, shards(): lax.ppermute(result, 'section', [(i, (i - 1) % count) for i in range(coun...  5.67 us
    ppermute x1, starting transfers between devices, shards(): other = lax.ppermute(own, 'dp', swap)  1.86 us
  transfers between devices with their start and end apart: 5, of which 1 were waited for; matrix products, arithmetic and copies ran while one was open for 0% of the time, Pallas kernels for 11%

profile of v3, /device:TPU:1, one launch (start us, length us, event | category | flops | bytes accessed | tf_op | source)
XLA Modules:
  0.0 57.6 jit_solution(390973534570355813)
XLA Ops:
  0.7 1.4 %shard_map.130 = (bf16[16,208,128]{2,1,0:T(8,128)(2,1)S(1)}, bf16[256,2048]{1,0:T(8,128)(2,1)S(1)}) custom-call(s32[1]{0:T(128)} %bitcast.column, s32[1]{0:T(128)} %bitcast.1.block, s32[1,4]{1,0:T(1,128)} %lengths.1, bf16[128,128]{1,0:T(8,128)(2,1)} %bitcast.22, bf16[128,128]{1,0:T(8,128)(2,1)} %bitcast.25, s32[2,128]{1,0:T(2,128)} %bitcast.32, ...), custom_call_target="tpu_custom_call" | custom-call | tf_op jit(solution)/shard_map/pallas_call | solution.py:291
  2.1 21.3 %all_to_all.10.own_ref = bf16[16,208,128]{2,1,0:T(8,128)(2,1)S(1)} all-to-all(bf16[16,208,128]{2,1,0:T(8,128)(2,1)S(1)} %get-tuple-element.24), channel_id=1, replica_groups=mesh['section'=8,'expert_0'=4,'expert_1'=4,'dp'=2] {'expert_1','expert_0'}, dimensions={0} | all-to-all | bytes 1703936 | tf_op jit(solution)/shard_map/all_to_all | solution.py:322
  23.3 1.9 %collective-permute-start = (bf16[16,208,128]{2,1,0:T(8,128)(2,1)S(1)}, bf16[16,208,128]{2,1,0:T(8,128)(2,1)S(1)}, u32[]{:S(2)}, u32[]{:S(2)}) collective-permute-start(bf16[16,208,128]{2,1,0:T(8,128)(2,1)S(1)} %all_to_all.10.own_ref), channel_id=1, source_target_pairs={{0,1},{1,0},{2,3},{3,2},{4,5},{5,4},{6,7},{7,6},{8,9},{9,8},{10,11... | collective-permute-start | bytes 2555912 | tf_op jit(solution)/shard_map/ppermute | solution.py:323
  25.2 0.0 collective-permute-start.1
  25.2 0.5 collective-permute-start.2
  25.7 3.9 %shard_map.131 = (f32[1,2048]{1,0:T(1,128)S(1)}, bf16[2048,896]{1,0:T(8,128)(2,1)S(1)}, bf16[2048,896]{1,0:T(8,128)(2,1)S(1)}, bf16[640,2048]{1,0:T(8,128)(2,1)S(1)}) custom-call(f32[1,2048]{1,0:T(1,128)} %gain_ref.5, bf16[2048,896]{1,0:T(8,128)(2,1)} %bitcast.36, bf16[2048,896]{1,0:T(8,128)(2,1)} %bitcast.37, bf16[896,2048]{1,0:T(8,128)(2,1)} %bitcast.35), custom_call_target="tpu_custom_call" | custom-call | tf_op jit(solution)/shard_map/pallas_call | solution.py:291
  29.7 0.0 collective-permute-done.1.xo_ref
  29.7 0.0 collective-permute-done.2.go_ref
  29.7 0.0 collective-permute-done.other_ref
  29.7 0.0 copy-start.2
  29.7 0.0 copy-start.3
  29.7 0.0 copy-start.4
  29.7 0.0 copy-start.5
  29.7 0.0 copy-start.6
  29.8 5.4 %shard_map.132 = (f32[16,96,128]{2,1,0:T(8,128)S(1)}, bf16[16,96,128]{2,1,0:T(8,128)(2,1)S(1)}) custom-call(bf16[16,208,128]{2,1,0:T(8,128)(2,1)S(1)} %all_to_all.10.own_ref, bf16[16,208,128]{2,1,0:T(8,128)(2,1)S(1)} %collective-permute-done.other_ref, f32[1,2048]{1,0:T(1,128)S(1)} %get-tuple-element.26.gain_ref, ...), custom_call_target="tpu_custom_call" | custom-call | tf_op jit(solution)/shard_map/pallas_call | solution.py:291
  35.2 0.2 collective-permute-start.3
  35.4 2.1 %shard_map.133 = (f32[64,128]{1,0:T(8,128)}, f32[64,128]{1,0:T(8,128)}, f32[128,128]{1,0:T(8,128)S(1)}, f32[128,128]{1,0:T(8,128)S(1)}, f32[128,128]{1,0:T(8,128...) custom-call(s32[1]{0:T(128)} %bitcast.column, ...), custom_call_target="tpu_custom_call" | custom-call | tf_op jit(solution)/shard_map/pallas_call | solution.py:291
  37.5 0.0 collective-permute-done.3
  37.5 0.1 add_convert_fusion
  37.6 12.4 %all_to_all.11.in_ref = bf16[16,96,128]{2,1,0:T(8,128)(2,1)S(1)} all-to-all(bf16[16,96,128]{2,1,0:T(8,128)(2,1)S(1)} %add_convert_fusion), channel_id=1, replica_groups=mesh['section'=8,'expert_0'=4,'expert_1'=4,'dp'=2] {'expert_1','expert_0'}, dimensions={0} | all-to-all | bytes 786432 | tf_op jit(solution)/shard_map/all_to_all | solution.py:362
  50.0 0.3 shard_map.134
  50.3 5.7 %collective-permute-start.4 = (bf16[128,128]{1,0:T(8,128)(2,1)S(1)}, bf16[128,128]{1,0:T(8,128)(2,1)S(1)}, u32[]{:S(2)}, u32[]{:S(2)}) collective-permute-start(bf16[128,128]{1,0:T(8,128)(2,1)S(1)} %shard_map.134), channel_id=1, source_target_pairs={{0,224},{32,0},{64,32},{96,64},{128,96},{160,128},{192,160},{224,1... | collective-permute-start | bytes 98312 | tf_op jit(solution)/shard_map/ppermute | solution.py:370
  56.0 1.0 %collective-permute-done.4 = bf16[128,128]{1,0:T(8,128)(2,1)S(1)} collective-permute-done((bf16[128,128]{1,0:T(8,128)(2,1)S(1)}, bf16[128,128]{1,0:T(8,128)(2,1)S(1)}, u32[]{:S(2)}, u32[]{:S(2)}) %collective-permute-start.4) | collective-permute-done | bytes 32800 | tf_op jit(solution)/shard_map/ppermute | solution.py:370
  57.0 0.6 %copy.15 = bf16[1,128,128]{2,1,0:T(8,128)(2,1)} copy(bf16[1,128,128]{2,1,0:T(8,128)(2,1)S(1)} %bitcast.38) | data formatting | bytes 65536
  (9 shorter events, 0.0 us)
Async XLA Ops:
  0.6 24.6 %copy-start = (bf16[1,128,128]{2,1,0:T(8,128)(2,1)S(1)}, bf16[1,128,128]{2,1,0:T(8,128)(2,1)}, u32[]{:S(2)}) copy-start(bf16[1,128,128]{2,1,0:T(8,128)(2,1)} %param.11) | copy-start | bytes 98308
  0.6 24.6 %copy-start.1 = (bf16[1,128,128]{2,1,0:T(8,128)(2,1)S(1)}, bf16[1,128,128]{2,1,0:T(8,128)(2,1)}, u32[]{:S(2)}) copy-start(bf16[1,128,128]{2,1,0:T(8,128)(2,1)} %param.12) | copy-start | bytes 98308
  23.3 6.3 %collective-permute-start = (bf16[16,208,128]{2,1,0:T(8,128)(2,1)S(1)}, bf16[16,208,128]{2,1,0:T(8,128)(2,1)S(1)}, u32[]{:S(2)}, u32[]{:S(2)}) collective-permute-start(bf16[16,208,128]{2,1,0:T(8,128)(2,1)S(1)} %all_to_all.10.own_ref), channel_id=1, source_target_pairs={{0,1},{1,0},{2,3},{3,2},{4,5},{5,4},{6,7},{7,6},{8,9},{9,8},{10,11... | collective-permute-start | bytes 2555912 | tf_op jit(solution)/shard_map/ppermute | solution.py:323
  25.2 4.5 %collective-permute-start.1 = (bf16[128,128]{1,0:T(8,128)(2,1)S(1)}, bf16[128,128]{1,0:T(8,128)(2,1)S(1)}, u32[]{:S(2)}, u32[]{:S(2)}) collective-permute-start(bf16[128,128]{1,0:T(8,128)(2,1)S(1)} %bitcast.23), channel_id=1, source_target_pairs={{0,1},{1,0},{2,3},{3,2},{4,5},{5,4},{6,7},{7,6},{8,9},{9,8},{10,11... | collective-permute-start | bytes 98312 | tf_op jit(solution)/shard_map/ppermute | solution.py:309
  25.2 4.5 %collective-permute-start.2 = (bf16[128,128]{1,0:T(8,128)(2,1)S(1)}, bf16[128,128]{1,0:T(8,128)(2,1)S(1)}, u32[]{:S(2)}, u32[]{:S(2)}) collective-permute-start(bf16[128,128]{1,0:T(8,128)(2,1)S(1)} %bitcast.26), channel_id=1, source_target_pairs={{0,1},{1,0},{2,3},{3,2},{4,5},{5,4},{6,7},{7,6},{8,9},{9,8},{10,11... | collective-permute-start | bytes 98312 | tf_op jit(solution)/shard_map/ppermute | solution.py:310
  29.7 5.7 %copy-start.2 = (f32[1,2048]{1,0:T(1,128)S(1)}, f32[1,2048]{1,0:T(1,128)}, u32[]{:S(2)}) copy-start(f32[1,2048]{1,0:T(1,128)} %gain_ref.5) | copy-start | bytes 24580
  29.7 5.7 %copy-start.3 = (bf16[1,2048,4]{1,2,0:T(4,128)(2,1)S(1)}, bf16[1,2048,4]{1,2,0:T(4,128)(2,1)}, u32[]{:S(2)}) copy-start(bf16[1,2048,4]{1,2,0:T(4,128)(2,1)} %param.16) | copy-start | bytes 49156
  29.7 5.6 %copy-start.4 = (bf16[1,128,64]{1,2,0:T(8,128)(2,1)S(1)}, bf16[1,128,64]{1,2,0:T(8,128)(2,1)}, u32[]{:S(2)}) copy-start(bf16[1,128,64]{1,2,0:T(8,128)(2,1)} %param.20) | copy-start | bytes 49156
  29.7 5.6 %copy-start.5 = (s32[1,128,2]{1,2,0:T(2,128)S(1)}, s32[1,128,2]{1,2,0:T(2,128)}, u32[]{:S(2)}) copy-start(s32[1,128,2]{1,2,0:T(2,128)} %param.13) | copy-start | bytes 3076
  29.7 5.6 %copy-start.6 = (s32[1,4]{1,0:T(1,128)S(1)}, s32[1,4]{1,0:T(1,128)}, u32[]{:S(2)}) copy-start(s32[1,4]{1,0:T(1,128)} %lengths.1) | copy-start | bytes 52
  35.2 2.4 %collective-permute-start.3 = (bf16[16,96,128]{2,1,0:T(8,128)(2,1)S(1)}, bf16[16,96,128]{2,1,0:T(8,128)(2,1)S(1)}, u32[]{:S(2)}, u32[]{:S(2)}) collective-permute-start(bf16[16,96,128]{2,1,0:T(8,128)(2,1)S(1)} %get-tuple-element.32), channel_id=1, source_target_pairs={{0,1},{1,0},{2,3},{3,2},{4,5},{5,4},{6,7},{7,6},{8,9},{9,8},{10,11... | collective-permute-start | bytes 1179656 | tf_op jit(solution)/shard_map/ppermute | solution.py:348
  50.3 6.7 %collective-permute-start.4 = (bf16[128,128]{1,0:T(8,128)(2,1)S(1)}, bf16[128,128]{1,0:T(8,128)(2,1)S(1)}, u32[]{:S(2)}, u32[]{:S(2)}) collective-permute-start(bf16[128,128]{1,0:T(8,128)(2,1)S(1)} %shard_map.134), channel_id=1, source_target_pairs={{0,224},{32,0},{64,32},{96,64},{128,96},{160,128},{192,160},{224,1... | collective-permute-start | bytes 98312 | tf_op jit(solution)/shard_map/ppermute | solution.py:370

commit v4 on v3

--- a/solution.py
+++ b/solution.py
@@ -68,9 +68,9 @@
 
 
 def prepare_kernel(column, block, *refs):
-    sources, wd_hbm, out_ref, early_ref, sem = refs[:8], refs[8], refs[9], refs[10], refs[19]
-    lengths, x_ref, g_ref, routes_ref, gain_ref, router_ref, down_ref, up_ref = refs[11:19]
-    copies = [pltpu.make_async_copy(a, b, sem.at[i]) for i, (a, b) in enumerate(zip(sources, refs[11:19]))]
+    sources, wd_hbm, out_ref, early_ref, pair_ref, sem = refs[:8], refs[8], refs[9], refs[10], refs[11], refs[20]
+    lengths, x_ref, g_ref, routes_ref, gain_ref, router_ref, down_ref, up_ref = refs[12:20]
+    copies = [pltpu.make_async_copy(a, b, sem.at[i]) for i, (a, b) in enumerate(zip(sources, refs[12:20]))]
     early = []
     for k in range(EARLY // 128):
         rows = slice(k * 128, (k + 1) * 128)
@@ -83,6 +83,8 @@
         copy.wait()
     x = x_ref[...]
     g = g_ref[...]
+    pair_ref[0] = x
+    pair_ref[1] = g
     _, member, rank = members(routes_ref[...])
     slot = lax.broadcasted_iota(jnp.int32, (CAP, TOK), 0)
     place = jnp.where(member, rank.astype(jnp.int32), -1)
@@ -187,14 +189,14 @@
 
 
 def stats_kernel(
-    column, block, lengths, own_ref, other_ref, x_ref, g_ref, xo_ref, go_ref, routes_ref, gain_ref, down_ref, router_ref,
+    column, block, lengths, own_ref, other_ref, x_ref, g_ref, pair_ref, routes_ref, gain_ref, down_ref, router_ref,
     grad_down_ref, grad_up_ref, side_ref, base_ref, sb_ref, take_ref, hits_ref, routed_ref,
 ):
     grad_down = jnp.zeros((JOBS * RANK, COLS), F32)
     grad_up = jnp.zeros((JOBS * RANK, COLS), F32)
     gain = local_columns(gain_ref, column[0])
     row = lax.broadcasted_iota(jnp.int32, (8, TOK), 0)
-    for d, (ref, xr, gr) in enumerate(((own_ref, x_ref, g_ref), (other_ref, xo_ref, go_ref))):
+    for d, (ref, xr, gr) in enumerate(((own_ref, x_ref, g_ref), (other_ref, pair_ref.at[0], pair_ref.at[1]))):
         total = ref[0, 2 * CAP :, :].astype(F32)
         for c in range(1, GROUPS):
             total = total + ref[c, 2 * CAP :, :].astype(F32)
@@ -306,12 +308,10 @@
     column = lax.axis_index(EXPERT).astype(jnp.int32).reshape(1)
     block = lax.axis_index("dp").astype(jnp.int32).reshape(1)
     swap = [(0, 1), (1, 0)]
-    xo = lax.ppermute(x, "dp", swap)
-    go = lax.ppermute(g, "dp", swap)
     locals_ = (lengths, x, g, routes, gains, router, down, up)
-    sent, early = call(
+    sent, early, pair = call(
         prepare_kernel,
-        (shape((GROUPS, SEND, 128), BF16), shape((EARLY, MODEL_WIDTH), BF16)),
+        (shape((GROUPS, SEND, 128), BF16), shape((EARLY, MODEL_WIDTH), BF16), shape((2, TOK, COLS), BF16)),
         (column, block),
         (*locals_, wd),
         [pltpu.SMEM(lengths.shape, jnp.int32)]
@@ -332,7 +332,7 @@
         [pltpu.SemaphoreType.DMA((3, 4)), pltpu.SemaphoreType.DMA],
         [HBM] * 4,
     )
-    other, xo, go = lax.optimization_barrier((other, xo, go))
+    other, pair = lax.optimization_barrier((other, lax.ppermute(pair, "dp", swap)))
     own_part, other_part = call(
         expert_kernel,
         (shape((GROUPS, BACK, 128), F32), shape((GROUPS, BACK, 128), BF16)),
@@ -355,7 +355,7 @@
             shape((2, EXPERTS, TOK, 128), BF16), shape((2, EXPERTS, TOK, 128), F32), square,
         ),
         (column, block, lengths),
-        (own, other, x, g, xo, go, routes, gains, down, router),
+        (own, other, x, g, pair, routes, gains, down, router),
     )
     arrived, side = lax.optimization_barrier((arrived, side))
     parts = (own_part + arrived.astype(F32)).astype(BF16)

time: 57.8 us -> 57.7 us (level)
  transfers between devices with their start and end apart: 5 -> 4, of which waited for: 1 -> 1; matrix products, arithmetic and copies ran while one was open for 0% -> 0% of each run, Pallas kernels for 11% -> 11%
where the time goes in v4:
time: 57.7 us; the launch traced here: 57.5 us
  blocking collectives  33.6 us (58%)
  Pallas kernels  13.2 us (23%)
  starting transfers between devices  8.1 us (14%)
  waiting for transfers between devices  1.03 us (2%)
  between operations  0.78 us (1%)
  local copies, waits for them, and re-layouts  0.66 us (1%)
    all_to_all x1, blocking collectives, shards(): own = lax.all_to_all(sent, EXCHANGE, 0, 0, tiled=True)  21.3 us
    pallas_call x5, Pallas kernels, call(): pl.pallas_call(kernel, in_specs=[SMEM] * len(scalars) + (arg_specs or [VM...  13.2 us
    all_to_all x1, blocking collectives, shards(): back = lax.all_to_all(parts, EXCHANGE, 0, 0, tiled=True)  12.4 us
    ppermute x1, starting transfers between devices, shards(): lax.ppermute(result, 'section', [(i, (i - 1) % count) for i in range(coun...  5.64 us
    ppermute x1, starting transfers between devices, shards(): other = lax.ppermute(own, 'dp', swap)  1.86 us
  transfers between devices with their start and end apart: 4, of which 1 were waited for; matrix products, arithmetic and copies ran while one was open for 0% of the time, Pallas kernels for 11%

profile of v4, /device:TPU:1, one launch (start us, length us, event | category | flops | bytes accessed | tf_op | source)
XLA Modules:
  0.0 57.5 jit_solution(2319794818852430225)
XLA Ops:
  0.6 1.4 %shard_map.130 = (bf16[16,208,128]{2,1,0:T(8,128)(2,1)S(1)}, bf16[256,2048]{1,0:T(8,128)(2,1)S(1)}, bf16[2,128,128]{2,1,0:T(8,128)(2,1)S(1)}) custom-call(s32[1]{0:T(128)} %bitcast.column, s32[1]{0:T(128)} %bitcast.1.block, s32[1,4]{1,0:T(1,128)} %lengths.1, bf16[128,128]{1,0:T(8,128)(2,1)} %bitcast.22, bf16[128,128]{1,0:T(8,128)(2,1)} %bitcast.24, ...), custom_call_target="tpu_custom_call" | custom-call | tf_op jit(solution)/shard_map/pallas_call | solution.py:293
  2.1 21.3 %all_to_all.10.own_ref = bf16[16,208,128]{2,1,0:T(8,128)(2,1)S(1)} all-to-all(bf16[16,208,128]{2,1,0:T(8,128)(2,1)S(1)} %get-tuple-element.24), channel_id=1, replica_groups=mesh['section'=8,'expert_0'=4,'expert_1'=4,'dp'=2] {'expert_1','expert_0'}, dimensions={0} | all-to-all | bytes 1703936 | tf_op jit(solution)/shard_map/all_to_all | solution.py:322
  23.3 1.9 %collective-permute-start = (bf16[16,208,128]{2,1,0:T(8,128)(2,1)S(1)}, bf16[16,208,128]{2,1,0:T(8,128)(2,1)S(1)}, u32[]{:S(2)}, u32[]{:S(2)}) collective-permute-start(bf16[16,208,128]{2,1,0:T(8,128)(2,1)S(1)} %all_to_all.10.own_ref), channel_id=1, source_target_pairs={{0,1},{1,0},{2,3},{3,2},{4,5},{5,4},{6,7},{7,6},{8,9},{9,8},{10,11... | collective-permute-start | bytes 2555912 | tf_op jit(solution)/shard_map/ppermute | solution.py:323
  25.2 0.0 collective-permute-start.1
  25.2 3.9 %shard_map.131 = (f32[1,2048]{1,0:T(1,128)S(1)}, bf16[2048,896]{1,0:T(8,128)(2,1)S(1)}, bf16[2048,896]{1,0:T(8,128)(2,1)S(1)}, bf16[640,2048]{1,0:T(8,128)(2,1)S(1)}) custom-call(f32[1,2048]{1,0:T(1,128)} %gain_ref.5, bf16[2048,896]{1,0:T(8,128)(2,1)} %bitcast.34, bf16[2048,896]{1,0:T(8,128)(2,1)} %bitcast.35, bf16[896,2048]{1,0:T(8,128)(2,1)} %bitcast.33), custom_call_target="tpu_custom_call" | custom-call | tf_op jit(solution)/shard_map/pallas_call | solution.py:293
  29.1 0.0 collective-permute-done.1.pair_ref
  29.1 0.0 collective-permute-done.other_ref
  29.2 0.0 copy-start
  29.2 0.0 copy-start.1
  29.2 0.0 copy-start.2
  29.2 0.0 copy-start.3
  29.2 0.0 copy-start.4
  29.2 0.0 copy-start.5
  29.2 0.0 copy-start.6
  29.2 5.4 %shard_map.132 = (f32[16,96,128]{2,1,0:T(8,128)S(1)}, bf16[16,96,128]{2,1,0:T(8,128)(2,1)S(1)}) custom-call(bf16[16,208,128]{2,1,0:T(8,128)(2,1)S(1)} %all_to_all.10.own_ref, bf16[16,208,128]{2,1,0:T(8,128)(2,1)S(1)} %collective-permute-done.other_ref, f32[1,2048]{1,0:T(1,128)S(1)} %get-tuple-element.27.gain_ref, ...), custom_call_target="tpu_custom_call" | custom-call | tf_op jit(solution)/shard_map/pallas_call | solution.py:293
  34.7 0.6 %collective-permute-start.2 = (bf16[16,96,128]{2,1,0:T(8,128)(2,1)S(1)}, bf16[16,96,128]{2,1,0:T(8,128)(2,1)S(1)}, u32[]{:S(2)}, u32[]{:S(2)}) collective-permute-start(bf16[16,96,128]{2,1,0:T(8,128)(2,1)S(1)} %get-tuple-element.33), channel_id=1, source_target_pairs={{0,1},{1,0},{2,3},{3,2},{4,5},{5,4},{6,7},{7,6},{8,9},{9,8},{10,11... | collective-permute-start | bytes 1179656 | tf_op jit(solution)/shard_map/ppermute | solution.py:348
  35.3 2.1 %shard_map.133 = (f32[64,128]{1,0:T(8,128)}, f32[64,128]{1,0:T(8,128)}, f32[128,128]{1,0:T(8,128)S(1)}, f32[128,128]{1,0:T(8,128)S(1)}, f32[128,128]{1,0:T(8,128...) custom-call(s32[1]{0:T(128)} %bitcast.column, ...), custom_call_target="tpu_custom_call" | custom-call | tf_op jit(solution)/shard_map/pallas_call | solution.py:293
  37.4 0.0 collective-permute-done.2
  37.4 0.1 add_convert_fusion
  37.5 12.4 %all_to_all.11.in_ref = bf16[16,96,128]{2,1,0:T(8,128)(2,1)S(1)} all-to-all(bf16[16,96,128]{2,1,0:T(8,128)(2,1)S(1)} %add_convert_fusion), channel_id=1, replica_groups=mesh['section'=8,'expert_0'=4,'expert_1'=4,'dp'=2] {'expert_1','expert_0'}, dimensions={0} | all-to-all | bytes 786432 | tf_op jit(solution)/shard_map/all_to_all | solution.py:362
  49.9 0.3 shard_map.134
  50.3 5.6 %collective-permute-start.3 = (bf16[128,128]{1,0:T(8,128)(2,1)S(1)}, bf16[128,128]{1,0:T(8,128)(2,1)S(1)}, u32[]{:S(2)}, u32[]{:S(2)}) collective-permute-start(bf16[128,128]{1,0:T(8,128)(2,1)S(1)} %shard_map.134), channel_id=1, source_target_pairs={{0,224},{32,0},{64,32},{96,64},{128,96},{160,128},{192,160},{224,1... | collective-permute-start | bytes 98312 | tf_op jit(solution)/shard_map/ppermute | solution.py:370
  55.9 1.0 %collective-permute-done.3 = bf16[128,128]{1,0:T(8,128)(2,1)S(1)} collective-permute-done((bf16[128,128]{1,0:T(8,128)(2,1)S(1)}, bf16[128,128]{1,0:T(8,128)(2,1)S(1)}, u32[]{:S(2)}, u32[]{:S(2)}) %collective-permute-start.3) | collective-permute-done | bytes 32800 | tf_op jit(solution)/shard_map/ppermute | solution.py:370
  56.9 0.6 %copy.15 = bf16[1,128,128]{2,1,0:T(8,128)(2,1)} copy(bf16[1,128,128]{2,1,0:T(8,128)(2,1)S(1)} %bitcast.36) | data formatting | bytes 65536
  (7 shorter events, 0.0 us)
Async XLA Ops:
  23.3 5.8 %collective-permute-start = (bf16[16,208,128]{2,1,0:T(8,128)(2,1)S(1)}, bf16[16,208,128]{2,1,0:T(8,128)(2,1)S(1)}, u32[]{:S(2)}, u32[]{:S(2)}) collective-permute-start(bf16[16,208,128]{2,1,0:T(8,128)(2,1)S(1)} %all_to_all.10.own_ref), channel_id=1, source_target_pairs={{0,1},{1,0},{2,3},{3,2},{4,5},{5,4},{6,7},{7,6},{8,9},{9,8},{10,11... | collective-permute-start | bytes 2555912 | tf_op jit(solution)/shard_map/ppermute | solution.py:323
  25.2 4.0 %collective-permute-start.1 = (bf16[2,128,128]{2,1,0:T(8,128)(2,1)S(1)}, bf16[2,128,128]{2,1,0:T(8,128)(2,1)S(1)}, u32[]{:S(2)}, u32[]{:S(2)}) collective-permute-start(bf16[2,128,128]{2,1,0:T(8,128)(2,1)S(1)} %get-tuple-element.25), channel_id=1, source_target_pairs={{0,1},{1,0},{2,3},{3,2},{4,5},{5,4},{6,7},{7,6},{8,9},{9,8},{10,11... | collective-permute-start | bytes 196616 | tf_op jit(solution)/shard_map/ppermute | solution.py:335
  29.2 6.1 %copy-start = (bf16[1,128,128]{2,1,0:T(8,128)(2,1)S(1)}, bf16[1,128,128]{2,1,0:T(8,128)(2,1)}, u32[]{:S(2)}) copy-start(bf16[1,128,128]{2,1,0:T(8,128)(2,1)} %param.11) | copy-start | bytes 98308
  29.2 6.1 %copy-start.1 = (bf16[1,128,128]{2,1,0:T(8,128)(2,1)S(1)}, bf16[1,128,128]{2,1,0:T(8,128)(2,1)}, u32[]{:S(2)}) copy-start(bf16[1,128,128]{2,1,0:T(8,128)(2,1)} %param.12) | copy-start | bytes 98308
  29.2 6.1 %copy-start.2 = (f32[1,2048]{1,0:T(1,128)S(1)}, f32[1,2048]{1,0:T(1,128)}, u32[]{:S(2)}) copy-start(f32[1,2048]{1,0:T(1,128)} %gain_ref.5) | copy-start | bytes 24580
  29.2 6.1 %copy-start.3 = (bf16[1,2048,4]{1,2,0:T(4,128)(2,1)S(1)}, bf16[1,2048,4]{1,2,0:T(4,128)(2,1)}, u32[]{:S(2)}) copy-start(bf16[1,2048,4]{1,2,0:T(4,128)(2,1)} %param.16) | copy-start | bytes 49156
  29.2 6.1 %copy-start.4 = (bf16[1,128,64]{1,2,0:T(8,128)(2,1)S(1)}, bf16[1,128,64]{1,2,0:T(8,128)(2,1)}, u32[]{:S(2)}) copy-start(bf16[1,128,64]{1,2,0:T(8,128)(2,1)} %param.20) | copy-start | bytes 49156
  29.2 6.1 %copy-start.5 = (s32[1,128,2]{1,2,0:T(2,128)S(1)}, s32[1,128,2]{1,2,0:T(2,128)}, u32[]{:S(2)}) copy-start(s32[1,128,2]{1,2,0:T(2,128)} %param.13) | copy-start | bytes 3076
  29.2 6.1 %copy-start.6 = (s32[1,4]{1,0:T(1,128)S(1)}, s32[1,4]{1,0:T(1,128)}, u32[]{:S(2)}) copy-start(s32[1,4]{1,0:T(1,128)} %lengths.1) | copy-start | bytes 52
  34.7 2.8 %collective-permute-start.2 = (bf16[16,96,128]{2,1,0:T(8,128)(2,1)S(1)}, bf16[16,96,128]{2,1,0:T(8,128)(2,1)S(1)}, u32[]{:S(2)}, u32[]{:S(2)}) collective-permute-start(bf16[16,96,128]{2,1,0:T(8,128)(2,1)S(1)} %get-tuple-element.33), channel_id=1, source_target_pairs={{0,1},{1,0},{2,3},{3,2},{4,5},{5,4},{6,7},{7,6},{8,9},{9,8},{10,11... | collective-permute-start | bytes 1179656 | tf_op jit(solution)/shard_map/ppermute | solution.py:348
  50.3 6.7 %collective-permute-start.3 = (bf16[128,128]{1,0:T(8,128)(2,1)S(1)}, bf16[128,128]{1,0:T(8,128)(2,1)S(1)}, u32[]{:S(2)}, u32[]{:S(2)}) collective-permute-start(bf16[128,128]{1,0:T(8,128)(2,1)S(1)} %shard_map.134), channel_id=1, source_target_pairs={{0,224},{32,0},{64,32},{96,64},{128,96},{160,128},{192,160},{224,1... | collective-permute-start | bytes 98312 | tf_op jit(solution)/shard_map/ppermute | solution.py:370

commit v5 on v4

--- a/solution.py
+++ b/solution.py
@@ -18,7 +18,7 @@
 SEND = 2 * CAP + STATS
 BACK = CAP + 16
 HIDDEN = 896
-EARLY = 256
+EARLY = 512
 EXPERT = ("expert_0", "expert_1")
 EXCHANGE = ("expert_1", "expert_0")
 EXPERT_DP = ("expert_0", "expert_1", "dp")

time: 57.7 us -> 57.8 us (level)
  transfers between devices with their start and end apart: 4 -> 4, of which waited for: 1 -> 1; matrix products, arithmetic and copies ran while one was open for 0% -> 0% of each run, Pallas kernels for 11% -> 10%
where the time goes in v5:
time: 57.8 us; the launch traced here: 57.6 us
  blocking collectives  33.6 us (58%)
  Pallas kernels  13.3 us (23%)
  starting transfers between devices  8.1 us (14%)
  waiting for transfers between devices  1.03 us (2%)
  between operations  0.78 us (1%)
  local copies, waits for them, and re-layouts  0.66 us (1%)
    all_to_all x1, blocking collectives, shards(): own = lax.all_to_all(sent, EXCHANGE, 0, 0, tiled=True)  21.3 us
    pallas_call x5, Pallas kernels, call(): pl.pallas_call(kernel, in_specs=[SMEM] * len(scalars) + (arg_specs or [VM...  13.3 us
    all_to_all x1, blocking collectives, shards(): back = lax.all_to_all(parts, EXCHANGE, 0, 0, tiled=True)  12.4 us
    ppermute x1, starting transfers between devices, shards(): lax.ppermute(result, 'section', [(i, (i - 1) % count) for i in range(coun...  5.65 us
    ppermute x1, starting transfers between devices, shards(): other = lax.ppermute(own, 'dp', swap)  1.86 us
  transfers between devices with their start and end apart: 4, of which 1 were waited for; matrix products, arithmetic and copies ran while one was open for 0% of the time, Pallas kernels for 10%

profile of v5, /device:TPU:1, one launch (start us, length us, event | category | flops | bytes accessed | tf_op | source)
XLA Modules:
  0.0 57.6 jit_solution(17256014644396645683)
XLA Ops:
  0.6 1.8 %shard_map.130 = (bf16[16,208,128]{2,1,0:T(8,128)(2,1)S(1)}, bf16[512,2048]{1,0:T(8,128)(2,1)S(1)}, bf16[2,128,128]{2,1,0:T(8,128)(2,1)S(1)}) custom-call(s32[1]{0:T(128)} %bitcast.column, s32[1]{0:T(128)} %bitcast.1.block, s32[1,4]{1,0:T(1,128)} %lengths.1, bf16[128,128]{1,0:T(8,128)(2,1)} %bitcast.22, bf16[128,128]{1,0:T(8,128)(2,1)} %bitcast.24, ...), custom_call_target="tpu_custom_call" | custom-call | tf_op jit(solution)/shard_map/pallas_call | solution.py:293
  2.4 21.3 %all_to_all.10.own_ref = bf16[16,208,128]{2,1,0:T(8,128)(2,1)S(1)} all-to-all(bf16[16,208,128]{2,1,0:T(8,128)(2,1)S(1)} %get-tuple-element.24), channel_id=1, replica_groups=mesh['section'=8,'expert_0'=4,'expert_1'=4,'dp'=2] {'expert_1','expert_0'}, dimensions={0} | all-to-all | bytes 1703936 | tf_op jit(solution)/shard_map/all_to_all | solution.py:322
  23.7 1.9 %collective-permute-start = (bf16[16,208,128]{2,1,0:T(8,128)(2,1)S(1)}, bf16[16,208,128]{2,1,0:T(8,128)(2,1)S(1)}, u32[]{:S(2)}, u32[]{:S(2)}) collective-permute-start(bf16[16,208,128]{2,1,0:T(8,128)(2,1)S(1)} %all_to_all.10.own_ref), channel_id=1, source_target_pairs={{0,1},{1,0},{2,3},{3,2},{4,5},{5,4},{6,7},{7,6},{8,9},{9,8},{10,11... | collective-permute-start | bytes 2555912 | tf_op jit(solution)/shard_map/ppermute | solution.py:323
  25.5 0.0 collective-permute-start.1
  25.5 3.6 %shard_map.131 = (f32[1,2048]{1,0:T(1,128)S(1)}, bf16[2048,896]{1,0:T(8,128)(2,1)S(1)}, bf16[2048,896]{1,0:T(8,128)(2,1)S(1)}, bf16[384,2048]{1,0:T(8,128)(2,1)S(1)}) custom-call(f32[1,2048]{1,0:T(1,128)} %gain_ref.5, bf16[2048,896]{1,0:T(8,128)(2,1)} %bitcast.34, bf16[2048,896]{1,0:T(8,128)(2,1)} %bitcast.35, bf16[896,2048]{1,0:T(8,128)(2,1)} %bitcast.33), custom_call_target="tpu_custom_call" | custom-call | tf_op jit(solution)/shard_map/pallas_call | solution.py:293
  29.2 0.0 collective-permute-done.1.pair_ref
  29.2 0.0 collective-permute-done.other_ref
  29.2 0.0 copy-start
  29.2 0.0 copy-start.1
  29.2 0.0 copy-start.2
  29.2 0.0 copy-start.3
  29.2 0.0 copy-start.4
  29.2 0.0 copy-start.5
  29.2 0.0 copy-start.6
  29.3 5.4 %shard_map.132 = (f32[16,96,128]{2,1,0:T(8,128)S(1)}, bf16[16,96,128]{2,1,0:T(8,128)(2,1)S(1)}) custom-call(bf16[16,208,128]{2,1,0:T(8,128)(2,1)S(1)} %all_to_all.10.own_ref, bf16[16,208,128]{2,1,0:T(8,128)(2,1)S(1)} %collective-permute-done.other_ref, f32[1,2048]{1,0:T(1,128)S(1)} %get-tuple-element.27.gain_ref, ...), custom_call_target="tpu_custom_call" | custom-call | tf_op jit(solution)/shard_map/pallas_call | solution.py:293
  34.7 0.6 %collective-permute-start.2 = (bf16[16,96,128]{2,1,0:T(8,128)(2,1)S(1)}, bf16[16,96,128]{2,1,0:T(8,128)(2,1)S(1)}, u32[]{:S(2)}, u32[]{:S(2)}) collective-permute-start(bf16[16,96,128]{2,1,0:T(8,128)(2,1)S(1)} %get-tuple-element.33), channel_id=1, source_target_pairs={{0,1},{1,0},{2,3},{3,2},{4,5},{5,4},{6,7},{7,6},{8,9},{9,8},{10,11... | collective-permute-start | bytes 1179656 | tf_op jit(solution)/shard_map/ppermute | solution.py:348
  35.3 2.1 %shard_map.133 = (f32[64,128]{1,0:T(8,128)}, f32[64,128]{1,0:T(8,128)}, f32[128,128]{1,0:T(8,128)S(1)}, f32[128,128]{1,0:T(8,128)S(1)}, f32[128,128]{1,0:T(8,128...) custom-call(s32[1]{0:T(128)} %bitcast.column, ...), custom_call_target="tpu_custom_call" | custom-call | tf_op jit(solution)/shard_map/pallas_call | solution.py:293
  37.4 0.0 collective-permute-done.2
  37.5 0.1 add_convert_fusion
  37.6 12.4 %all_to_all.11.in_ref = bf16[16,96,128]{2,1,0:T(8,128)(2,1)S(1)} all-to-all(bf16[16,96,128]{2,1,0:T(8,128)(2,1)S(1)} %add_convert_fusion), channel_id=1, replica_groups=mesh['section'=8,'expert_0'=4,'expert_1'=4,'dp'=2] {'expert_1','expert_0'}, dimensions={0} | all-to-all | bytes 786432 | tf_op jit(solution)/shard_map/all_to_all | solution.py:362
  49.9 0.3 shard_map.134
  50.3 5.6 %collective-permute-start.3 = (bf16[128,128]{1,0:T(8,128)(2,1)S(1)}, bf16[128,128]{1,0:T(8,128)(2,1)S(1)}, u32[]{:S(2)}, u32[]{:S(2)}) collective-permute-start(bf16[128,128]{1,0:T(8,128)(2,1)S(1)} %shard_map.134), channel_id=1, source_target_pairs={{0,224},{32,0},{64,32},{96,64},{128,96},{160,128},{192,160},{224,1... | collective-permute-start | bytes 98312 | tf_op jit(solution)/shard_map/ppermute | solution.py:370
  55.9 1.0 %collective-permute-done.3 = bf16[128,128]{1,0:T(8,128)(2,1)S(1)} collective-permute-done((bf16[128,128]{1,0:T(8,128)(2,1)S(1)}, bf16[128,128]{1,0:T(8,128)(2,1)S(1)}, u32[]{:S(2)}, u32[]{:S(2)}) %collective-permute-start.3) | collective-permute-done | bytes 32800 | tf_op jit(solution)/shard_map/ppermute | solution.py:370
  57.0 0.6 %copy.15 = bf16[1,128,128]{2,1,0:T(8,128)(2,1)} copy(bf16[1,128,128]{2,1,0:T(8,128)(2,1)S(1)} %bitcast.36) | data formatting | bytes 65536
  (7 shorter events, 0.0 us)
Async XLA Ops:
  23.7 5.5 %collective-permute-start = (bf16[16,208,128]{2,1,0:T(8,128)(2,1)S(1)}, bf16[16,208,128]{2,1,0:T(8,128)(2,1)S(1)}, u32[]{:S(2)}, u32[]{:S(2)}) collective-permute-start(bf16[16,208,128]{2,1,0:T(8,128)(2,1)S(1)} %all_to_all.10.own_ref), channel_id=1, source_target_pairs={{0,1},{1,0},{2,3},{3,2},{4,5},{5,4},{6,7},{7,6},{8,9},{9,8},{10,11... | collective-permute-start | bytes 2555912 | tf_op jit(solution)/shard_map/ppermute | solution.py:323
  25.5 3.6 %collective-permute-start.1 = (bf16[2,128,128]{2,1,0:T(8,128)(2,1)S(1)}, bf16[2,128,128]{2,1,0:T(8,128)(2,1)S(1)}, u32[]{:S(2)}, u32[]{:S(2)}) collective-permute-start(bf16[2,128,128]{2,1,0:T(8,128)(2,1)S(1)} %get-tuple-element.25), channel_id=1, source_target_pairs={{0,1},{1,0},{2,3},{3,2},{4,5},{5,4},{6,7},{7,6},{8,9},{9,8},{10,11... | collective-permute-start | bytes 196616 | tf_op jit(solution)/shard_map/ppermute | solution.py:335
  29.2 6.1 %copy-start = (bf16[1,128,128]{2,1,0:T(8,128)(2,1)S(1)}, bf16[1,128,128]{2,1,0:T(8,128)(2,1)}, u32[]{:S(2)}) copy-start(bf16[1,128,128]{2,1,0:T(8,128)(2,1)} %param.11) | copy-start | bytes 98308
  29.2 6.1 %copy-start.1 = (bf16[1,128,128]{2,1,0:T(8,128)(2,1)S(1)}, bf16[1,128,128]{2,1,0:T(8,128)(2,1)}, u32[]{:S(2)}) copy-start(bf16[1,128,128]{2,1,0:T(8,128)(2,1)} %param.12) | copy-start | bytes 98308
  29.2 6.1 %copy-start.2 = (f32[1,2048]{1,0:T(1,128)S(1)}, f32[1,2048]{1,0:T(1,128)}, u32[]{:S(2)}) copy-start(f32[1,2048]{1,0:T(1,128)} %gain_ref.5) | copy-start | bytes 24580
  29.2 6.1 %copy-start.3 = (bf16[1,2048,4]{1,2,0:T(4,128)(2,1)S(1)}, bf16[1,2048,4]{1,2,0:T(4,128)(2,1)}, u32[]{:S(2)}) copy-start(bf16[1,2048,4]{1,2,0:T(4,128)(2,1)} %param.16) | copy-start | bytes 49156
  29.2 6.1 %copy-start.4 = (bf16[1,128,64]{1,2,0:T(8,128)(2,1)S(1)}, bf16[1,128,64]{1,2,0:T(8,128)(2,1)}, u32[]{:S(2)}) copy-start(bf16[1,128,64]{1,2,0:T(8,128)(2,1)} %param.20) | copy-start | bytes 49156
  29.2 6.1 %copy-start.5 = (s32[1,128,2]{1,2,0:T(2,128)S(1)}, s32[1,128,2]{1,2,0:T(2,128)}, u32[]{:S(2)}) copy-start(s32[1,128,2]{1,2,0:T(2,128)} %param.13) | copy-start | bytes 3076
  29.2 6.1 %copy-start.6 = (s32[1,4]{1,0:T(1,128)S(1)}, s32[1,4]{1,0:T(1,128)}, u32[]{:S(2)}) copy-start(s32[1,4]{1,0:T(1,128)} %lengths.1) | copy-start | bytes 52
  34.7 2.8 %collective-permute-start.2 = (bf16[16,96,128]{2,1,0:T(8,128)(2,1)S(1)}, bf16[16,96,128]{2,1,0:T(8,128)(2,1)S(1)}, u32[]{:S(2)}, u32[]{:S(2)}) collective-permute-start(bf16[16,96,128]{2,1,0:T(8,128)(2,1)S(1)} %get-tuple-element.33), channel_id=1, source_target_pairs={{0,1},{1,0},{2,3},{3,2},{4,5},{5,4},{6,7},{7,6},{8,9},{9,8},{10,11... | collective-permute-start | bytes 1179656 | tf_op jit(solution)/shard_map/ppermute | solution.py:348
  50.3 6.7 %collective-permute-start.3 = (bf16[128,128]{1,0:T(8,128)(2,1)S(1)}, bf16[128,128]{1,0:T(8,128)(2,1)S(1)}, u32[]{:S(2)}, u32[]{:S(2)}) collective-permute-start(bf16[128,128]{1,0:T(8,128)(2,1)S(1)} %shard_map.134), channel_id=1, source_target_pairs={{0,224},{32,0},{64,32},{96,64},{128,96},{160,128},{192,160},{224,1... | collective-permute-start | bytes 98312 | tf_op jit(solution)/shard_map/ppermute | solution.py:370
